TPU v7x, 768 devices: a whole 4x8x12 slice. The times are simulated.
768 devices in a mesh: grp: 16 (over y_hi, x, core), sub: 48 (over z, y_lo).
Axes of the slice: x: 4, y: 8 (y_hi: 2, y_lo: 4; y = y_hi * 4 + y_lo), z: 12, core: 2. Of those that a mesh axis runs over, the one named last changes fastest.
Arguments:
- loads: float32 [768, 8, 1024], P(('grp', 'sub')), may hold values from -6 to 6
- schur: bfloat16 [768, 1024, 1024], P(('grp', 'sub')), may hold values from -0.1875 to 0.1875
- neumann: bfloat16 [768, 1024, 1024], P(('grp', 'sub')), may hold values from -0.1875 to 0.1875
- basis: float32 [768, 24, 1024], P(('grp', 'sub')), may hold values from -0.375 to 0.375
- coarse_index: int32 [768, 24], P(('grp', 'sub')), may hold values from 0 to 3071
- coarse_inverse: float32 [3072, 3072], P(('grp', 'sub')), may hold values from -1 to 3
Outputs:
- solution: float32 [768, 8, 1024], P(('grp', 'sub'))
- residual: float32 [768, 8, 1024], P(('grp', 'sub'))
All inputs are finite; a program needn't handle non-finite values.
Results may differ from a plain program's by a relative error of at most 0.00063.
Values sent between devices are 32-bit elements; how exact they have to be, the bound alone decides.
No kernel may reach another device: no remote copies, remote signals or barrier semaphores. Data moves between devices by JAX's collectives and lax.ppermute only.
A program may use at most 64 MiB of HBM per device.

v0:
```python
import jax
import jax.numpy as jnp
from jax import lax
from jax.sharding import PartitionSpec as P

RIM = 256


def with_halo(x, sides, width):
    for axis, dim in sides:
        peers, length = (lax.axis_size(axis), x.shape[dim])
        up = [(i, (i + 1) % peers) for i in range(peers - 1)]
        down = [(j, i) for i, j in up]
        last = lax.slice_in_dim(x, length - width, length, axis=dim)
        first = lax.slice_in_dim(x, 0, width, axis=dim)
        before = lax.ppermute(last, axis, up)
        after = lax.ppermute(first, axis, down)
        x = jnp.concatenate([before, x, after], axis=dim)
    return x


def cut_along(x, dim, peers):
    before, after = (x.shape[:dim], x.shape[dim + 1 :])
    return jnp.moveaxis(x.reshape(*before, peers, -1, *after), dim, 0)


def sum_at_owner(x, axis, dim):
    blocks = cut_along(x, dim, lax.axis_size(axis))
    arrived = lax.all_to_all(blocks, axis, split_axis=0, concat_axis=0, tiled=True)
    return arrived.sum(axis=0)


def total_of_pieces(x, axis):
    return lax.all_gather(x, axis).sum(0)


def from_everyone(x, axis):
    copies = jnp.broadcast_to(x, (lax.axis_size(axis), *x.shape))
    return lax.all_to_all(copies, axis, split_axis=0, concat_axis=0, tiled=True)


def taken_together(x, axis):
    return from_everyone(x, axis).sum(axis=0)


def local(loads, schur, neumann, basis, coarse_index, coarse_inverse):
    width = loads.shape[2]
    coarse_total = coarse_inverse.shape[1]
    high = lax.Precision.HIGHEST
    position = lax.axis_index("sub")
    final_index = lax.axis_size("sub") - 1
    columns = lax.broadcasted_iota(jnp.int32, (1, 1, width), 2)
    lower_rim = (columns < RIM) & (position > 0)
    upper_rim = (columns >= width - RIM) & (position < final_index)
    weights = jnp.where(lower_rim | upper_rim, 0.5, 1.0).astype(jnp.float32)
    selector = (
        coarse_index[0][:, None] == lax.broadcasted_iota(jnp.int32, (1, coarse_total), 1)
    ).astype(jnp.float32)

    def assemble(field):
        padded = with_halo(field, (("sub", 2),), RIM)
        from_left = padded[:, :, :RIM]
        from_right = padded[:, :, RIM + width :]
        middle = field[:, :, RIM : width - RIM]
        return jnp.concatenate(
            [field[:, :, :RIM] + from_left, middle, field[:, :, width - RIM :] + from_right], axis=2
        )

    force = assemble(loads)
    residual = force
    weighted = (weights * residual)[0]
    product = jnp.dot(weighted.astype(jnp.bfloat16), neumann[0], preferred_element_type=jnp.float32)
    neumann_part = 0.25 * weighted + 0.0625 * product
    coarse_terms = jnp.dot(weighted, basis[0].T, precision=high)
    partial_sums = jnp.dot(coarse_terms, selector, precision=high)
    grouped = sum_at_owner(partial_sums, "grp", 1)
    owned = sum_at_owner(grouped, "sub", 1)
    value_terms = jnp.dot(owned, coarse_inverse, precision=high)
    within = total_of_pieces(value_terms, "sub")
    coarse_value = taken_together(within, "grp")
    picked = jnp.dot(coarse_value, selector.T, precision=high)
    combined = neumann_part + jnp.dot(picked, basis[0], precision=high)
    solution = assemble(weights * combined[None])
    product = jnp.dot(
        solution[0].astype(jnp.bfloat16), schur[0], preferred_element_type=jnp.float32
    )
    residual = force - assemble((4.0 * solution[0] + product)[None])
    return (solution, residual)


def solution(mesh):
    in_specs = (
        P(("grp", "sub"), None, None),
        P(("grp", "sub"), None, None),
        P(("grp", "sub"), None, None),
        P(("grp", "sub"), None, None),
        P(("grp", "sub"), None),
        P(("grp", "sub"), None),
    )
    out_specs = (P(("grp", "sub"), None, None), P(("grp", "sub"), None, None))
    return jax.shard_map(local, mesh=mesh, in_specs=in_specs, out_specs=out_specs, check_vma=False)
```

profile of v0, /device:TPU:248, one launch (start us, length us, event | category | flops | bytes accessed | tf_op | source)
XLA Modules:
  0.0 382.6 jit_solution(8459726150903724401)
XLA Ops:
  7.2 0.0 copy-start
  7.2 0.0 all-gather.3.cloned.1.call-start
  7.2 0.9 fusion.50
  8.1 7.8 %collective-permute-start = (f32[1,8,256]{2,1,0:T(8,128)S(1)}, f32[1,8,256]{2,1,0:T(8,128)S(1)}, u32[]{:S(2)}, u32[]{:S(2)}) collective-permute-start(f32[1,8,256]{2,1,0:T(8,128)S(1)} %get-tuple-element.18), channel_id=1, source_target_pairs={{0,1},{1,2},{2,3},{3,4},{4,5},{5,6},{6,7},{7,8},{8,9},{9,10},{10,1... | collective-permute-start | bytes 24584 | tf_op jit(solution)/shard_map/ppermute | solution.py:16
  15.9 1.9 collective-permute-start.1
  17.9 0.7 fusion.48
  18.6 0.0 collective-permute-done
  18.6 6.8 %collective-permute-done.1 = f32[1,8,256]{2,1,0:T(8,128)S(1)} collective-permute-done((f32[1,8,256]{2,1,0:T(8,128)S(1)}, f32[1,8,256]{2,1,0:T(8,128)S(1)}, u32[]{:S(2)}, u32[]{:S(2)}) %collective-permute-start.1) | collective-permute-done | bytes 8224 | tf_op jit(solution)/shard_map/ppermute | solution.py:17
  25.4 0.7 slice_add_fusion.5
  26.1 1.1 fusion.25
  27.2 1.0 fusion.20
  28.1 0.1 reshape.164
  28.2 0.1 copy.16
  28.3 14.8 %all_to_all.15 = f32[16,8,192]{2,1,0:T(8,128)S(1)} all-to-all(f32[16,8,192]{2,1,0:T(8,128)S(1)} %bitcast.55), channel_id=1, replica_groups=mesh['grp'=16,'sub'=48] {'grp'}, dimensions={0} | all-to-all | bytes 196608 | tf_op jit(solution)/shard_map/all_to_all | solution.py:29
  43.1 0.1 copy.13
  43.2 22.4 %all_to_all.16 = f32[48,8,4]{1,2,0:T(4,128)S(1)} all-to-all(f32[48,8,4]{1,2,0:T(4,128)S(1)} %bitcast.56), channel_id=1, replica_groups=mesh['grp'=16,'sub'=48] {'sub'}, dimensions={0} | all-to-all | bytes 12288 | tf_op jit(solution)/shard_map/all_to_all | solution.py:29
  65.6 0.1 reduce_sum.37
  65.6 1.7 fusion.51
  67.4 0.0 all-gather.3.cloned.1.call-update
  67.4 227.4 %all-gather.3.cloned.1.call-done = f32[384,3072]{1,0:T(8,128)} async-done(((f32[8,3072]{1,0:T(8,128)}), f32[384,3072]{1,0:T(8,128)}) %all-gather.3.cloned.1.call-update) | async-done | bytes 4718608 | tf_op jit(solution)/shard_map/all_gather | solution.py:34
  294.7 2.6 bitcast_reduce_fusion
  297.3 0.1 broadcast_in_dim.17
  297.5 0.0 copy-start.4
  297.5 0.0 copy-start.2
  297.5 42.6 %all_to_all.17 = f32[16,8,3072]{2,1,0:T(8,128)} all-to-all(f32[16,8,3072]{2,1,0:T(8,128)S(1)} %broadcast_in_dim.17), channel_id=1, replica_groups=mesh['grp'=16,'sub'=48] {'grp'}, dimensions={0} | all-to-all | bytes 3145728 | tf_op jit(solution)/shard_map/all_to_all | solution.py:39
  340.1 1.5 reduce_sum.39
  341.6 0.0 copy-done.4
  341.6 0.0 copy-start.1
  341.6 0.3 fusion.19
  341.9 0.0 copy-done.2
  341.9 0.2 fusion.23
  342.1 0.0 copy-done
  342.1 0.4 fusion.16
  342.5 11.3 %collective-permute-start.2 = (f32[1,8,256]{2,1,0:T(8,128)S(1)}, f32[1,8,256]{2,1,0:T(8,128)S(1)}, u32[]{:S(2)}, u32[]{:S(2)}) collective-permute-start(f32[1,8,256]{2,1,0:T(8,128)S(1)} %get-tuple-element.14), channel_id=1, source_target_pairs={{0,1},{1,2},{2,3},{3,4},{4,5},{5,6},{6,7},{7,8},{8,9},{9,10},{10,1... | collective-permute-start | bytes 24584 | tf_op jit(solution)/shard_map/ppermute | solution.py:16
  353.8 1.9 collective-permute-start.3
  355.8 0.0 collective-permute-done.2
  355.8 7.5 %collective-permute-done.3 = f32[1,8,256]{2,1,0:T(8,128)S(1)} collective-permute-done((f32[1,8,256]{2,1,0:T(8,128)S(1)}, f32[1,8,256]{2,1,0:T(8,128)S(1)}, u32[]{:S(2)}, u32[]{:S(2)}) %collective-permute-start.3) | collective-permute-done | bytes 8224 | tf_op jit(solution)/shard_map/ppermute | solution.py:17
  363.3 0.0 copy-start.3
  363.3 0.0 copy-done.1
  363.3 0.4 fusion.27
  363.7 1.9 collective-permute-start.4
  365.6 3.9 %collective-permute-start.5 = (f32[1,8,256]{2,1,0:T(8,128)S(1)}, f32[1,8,256]{2,1,0:T(8,128)S(1)}, u32[]{:S(2)}, u32[]{:S(2)}) collective-permute-start(f32[1,8,256]{2,1,0:T(8,128)S(1)} %get-tuple-element.9), channel_id=1, source_target_pairs={{1,0},{2,1},{3,2},{4,3},{5,4},{6,5},{7,6},{8,7},{9,8},{10,9},{11,1... | collective-permute-start | bytes 24584 | tf_op jit(solution)/shard_map/ppermute | solution.py:17
  369.6 0.0 collective-permute-done.4
  369.6 5.5 %collective-permute-done.5 = f32[1,8,256]{2,1,0:T(8,128)S(1)} collective-permute-done((f32[1,8,256]{2,1,0:T(8,128)S(1)}, f32[1,8,256]{2,1,0:T(8,128)S(1)}, u32[]{:S(2)}, u32[]{:S(2)}) %collective-permute-start.5) | collective-permute-done | bytes 8224 | tf_op jit(solution)/shard_map/ppermute | solution.py:17
  375.1 0.6 maximum_subtract_fusion
  375.7 0.0 copy-done.3
  (10 shorter events, 0.1 us)
Async XLA Ops:
  7.2 335.0 %copy-start = (bf16[1,1024,1024]{2,1,0:T(8,128)(2,1)S(1)}, bf16[1,1024,1024]{2,1,0:T(8,128)(2,1)}, u32[]{:S(2)}) copy-start(bf16[1,1024,1024]{2,1,0:T(8,128)(2,1)} %param.8) | copy-start | bytes 6291460
  7.2 287.6 %all-gather.3.cloned.1.call-start = ((), (), s32[]{:S(2)}) async-start(), calls=%async_computation.3 | async-start | bytes 4816896 | tf_op jit(solution)/shard_map/all_gather | solution.py:34
  8.1 10.5 %collective-permute-start = (f32[1,8,256]{2,1,0:T(8,128)S(1)}, f32[1,8,256]{2,1,0:T(8,128)S(1)}, u32[]{:S(2)}, u32[]{:S(2)}) collective-permute-start(f32[1,8,256]{2,1,0:T(8,128)S(1)} %get-tuple-element.18), channel_id=1, source_target_pairs={{0,1},{1,2},{2,3},{3,4},{4,5},{5,6},{6,7},{7,8},{8,9},{9,10},{10,1... | collective-permute-start | bytes 24584 | tf_op jit(solution)/shard_map/ppermute | solution.py:16
  15.9 9.5 %collective-permute-start.1 = (f32[1,8,256]{2,1,0:T(8,128)S(1)}, f32[1,8,256]{2,1,0:T(8,128)S(1)}, u32[]{:S(2)}, u32[]{:S(2)}) collective-permute-start(f32[1,8,256]{2,1,0:T(8,128)S(1)} %get-tuple-element.19), channel_id=1, source_target_pairs={{1,0},{2,1},{3,2},{4,3},{5,4},{6,5},{7,6},{8,7},{9,8},{10,9},{11,1... | collective-permute-start | bytes 24584 | tf_op jit(solution)/shard_map/ppermute | solution.py:17
  297.5 44.1 %copy-start.4 = (s32[1,24]{1,0:T(1,128)S(1)}, s32[1,24]{1,0:T(1,128)}, u32[]{:S(2)}) copy-start(s32[1,24]{1,0:T(1,128)} %param.10) | copy-start | bytes 292
  297.5 44.4 %copy-start.2 = (f32[1,24,1024]{2,1,0:T(8,128)S(1)}, f32[1,24,1024]{2,1,0:T(8,128)}, u32[]{:S(2)}) copy-start(f32[1,24,1024]{2,1,0:T(8,128)} %param.9) | copy-start | bytes 294916
  341.6 21.7 %copy-start.1 = (bf16[1,1024,1024]{2,1,0:T(8,128)(2,1)S(1)}, bf16[1,1024,1024]{2,1,0:T(8,128)(2,1)}, u32[]{:S(2)}) copy-start(bf16[1,1024,1024]{2,1,0:T(8,128)(2,1)} %param.7) | copy-start | bytes 6291460
  342.5 13.3 %collective-permute-start.2 = (f32[1,8,256]{2,1,0:T(8,128)S(1)}, f32[1,8,256]{2,1,0:T(8,128)S(1)}, u32[]{:S(2)}, u32[]{:S(2)}) collective-permute-start(f32[1,8,256]{2,1,0:T(8,128)S(1)} %get-tuple-element.14), channel_id=1, source_target_pairs={{0,1},{1,2},{2,3},{3,4},{4,5},{5,6},{6,7},{7,8},{8,9},{9,10},{10,1... | collective-permute-start | bytes 24584 | tf_op jit(solution)/shard_map/ppermute | solution.py:16
  353.8 9.5 %collective-permute-start.3 = (f32[1,8,256]{2,1,0:T(8,128)S(1)}, f32[1,8,256]{2,1,0:T(8,128)S(1)}, u32[]{:S(2)}, u32[]{:S(2)}) collective-permute-start(f32[1,8,256]{2,1,0:T(8,128)S(1)} %get-tuple-element.15), channel_id=1, source_target_pairs={{1,0},{2,1},{3,2},{4,3},{5,4},{6,5},{7,6},{8,7},{9,8},{10,9},{11,1... | collective-permute-start | bytes 24584 | tf_op jit(solution)/shard_map/ppermute | solution.py:17
  363.3 12.4 %copy-start.3 = (f32[1,8,1024]{2,1,0:T(8,128)}, f32[1,8,1024]{2,1,0:T(8,128)S(1)}, u32[]{:S(2)}) copy-start(f32[1,8,1024]{2,1,0:T(8,128)S(1)} %pad_maximum_fusion) | copy-start | bytes 98308
  363.7 5.9 %collective-permute-start.4 = (f32[1,8,256]{2,1,0:T(8,128)S(1)}, f32[1,8,256]{2,1,0:T(8,128)S(1)}, u32[]{:S(2)}, u32[]{:S(2)}) collective-permute-start(f32[1,8,256]{2,1,0:T(8,128)S(1)} %get-tuple-element.8), channel_id=1, source_target_pairs={{0,1},{1,2},{2,3},{3,4},{4,5},{5,6},{6,7},{7,8},{8,9},{9,10},{10,1... | collective-permute-start | bytes 24584 | tf_op jit(solution)/shard_map/ppermute | solution.py:16
  365.6 9.5 %collective-permute-start.5 = (f32[1,8,256]{2,1,0:T(8,128)S(1)}, f32[1,8,256]{2,1,0:T(8,128)S(1)}, u32[]{:S(2)}, u32[]{:S(2)}) collective-permute-start(f32[1,8,256]{2,1,0:T(8,128)S(1)} %get-tuple-element.9), channel_id=1, source_target_pairs={{1,0},{2,1},{3,2},{4,3},{5,4},{6,5},{7,6},{8,7},{9,8},{10,9},{11,1... | collective-permute-start | bytes 24584 | tf_op jit(solution)/shard_map/ppermute | solution.py:17
Sparse Core Ops, SparseCore 0:
  67.5 227.1 all-gather.2
where the time goes:
time: 383 us
  waiting for transfers between devices  247 us (64%)
  blocking collectives  79.7 us (21%)
  starting transfers between devices  28.8 us (8%)
  between operations  14.2 us (4%)
  other arithmetic  5.51 us (1%)
  matrix products  5.02 us (1%)
    all_gather x1, waiting for transfers between devices, total_of_pieces(): return lax.all_gather(x, axis).sum(0)  227 us
    all_to_all x1, blocking collectives, from_everyone(): return lax.all_to_all(copies, axis, split_axis=0, concat_axis=0, tiled=True)  42.6 us
    all_to_all x2, blocking collectives, sum_at_owner(): lax.all_to_all(blocks, axis, split_axis=0, concat_axis=0, tiled=True)  37.1 us
    ppermute x3, starting transfers between devices, with_halo(): before = lax.ppermute(last, axis, up)  21 us
    ppermute x3, waiting for transfers between devices, with_halo(): after = lax.ppermute(first, axis, down)  19.8 us
    ppermute x3, starting transfers between devices, with_halo(): after = lax.ppermute(first, axis, down)  7.76 us
  transfers between devices with their start and end apart: 7, of which 4 were waited for; matrix products, arithmetic and copies ran while one was open for 0% of the time, Pallas kernels for 0%

commit v1 on v0

v1 whole, which is shorter than its diff:
```python
import jax
import jax.numpy as jnp
from jax import lax
from jax.sharding import Mesh, PartitionSpec as P

RIM = 256
ALL = ("yh", "x", "c", "z", "yl")
SIZES = (2, 4, 2, 12, 4)
CHAIN = ("z", "yl")
ROWS = ("yh", "x", "yl")
COLS = ("z", "c")
N_ROWS = 32
N_COLS = 24
LANES = 128


def exchange(x, axes):
    return lax.all_to_all(x, axes, split_axis=0, concat_axis=0, tiled=True)


def position_of(index):
    owner = index // 4
    group, member = owner // 48, owner % 48
    row_part = (group // 2) * 4 + member % 4
    col_part = (member // 4) * 2 + group % 2
    return row_part * LANES + col_part * 4 + index % 4


def local(loads, schur, neumann, basis, coarse_index, coarse_inverse):
    width = loads.shape[2]
    high = lax.Precision.HIGHEST
    peers = 48
    position = lax.axis_index(CHAIN)
    columns = lax.broadcasted_iota(jnp.int32, (1, width), 1)
    lower_rim = (columns < RIM) & (position > 0)
    upper_rim = (columns >= width - RIM) & (position < peers - 1)
    weights = jnp.where(lower_rim | upper_rim, 0.5, 1.0).astype(jnp.float32)
    up = [(i, i + 1) for i in range(peers - 1)]
    down = [(j, i) for i, j in up]

    def assemble(field):
        before = lax.ppermute(field[:, width - RIM :], CHAIN, up)
        after = lax.ppermute(field[:, :RIM], CHAIN, down)
        middle = field[:, RIM : width - RIM]
        return jnp.concatenate([field[:, :RIM] + before, middle, field[:, width - RIM :] + after], axis=1)

    index = coarse_index[0]
    owner_hot = (position_of(index)[:, None] == lax.broadcasted_iota(jnp.int32, (1, N_ROWS * LANES), 1)).astype(jnp.float32)
    value_hot = (index[:, None] == lax.broadcasted_iota(jnp.int32, (1, N_COLS * LANES), 1)).astype(jnp.float32)

    force = assemble(loads[0])
    weighted = weights * force
    product = jnp.dot(weighted.astype(jnp.bfloat16), neumann[0], preferred_element_type=jnp.float32)
    neumann_part = 0.25 * weighted + 0.0625 * product
    coarse_terms = jnp.dot(weighted, basis[0].T, precision=high)

    partial = jnp.dot(coarse_terms, owner_hot, precision=high)
    partial = partial.reshape(8, N_ROWS, LANES).transpose(1, 0, 2)
    part = exchange(partial, ROWS).sum(0)
    inverse = coarse_inverse.reshape(4, N_COLS, LANES).transpose(1, 0, 2)
    sent = jnp.concatenate(
        [jnp.broadcast_to(part, (N_COLS, 8, LANES)), inverse, jnp.zeros((N_COLS, 4, LANES), jnp.float32)], axis=1
    )
    arrived = exchange(sent, COLS)
    residual_rows = arrived[:, :8].sum(0)[:, : 4 * N_COLS]
    block = arrived[:, 8:12].reshape(4 * N_COLS, LANES)
    value_part = jnp.dot(residual_rows, block, precision=high)
    value_cols = exchange(jnp.broadcast_to(value_part, (N_ROWS, 8, LANES)), ROWS).sum(0)
    value = exchange(jnp.broadcast_to(value_cols, (N_COLS, 8, LANES)), COLS)
    value = value.transpose(1, 0, 2).reshape(8, N_COLS * LANES)
    picked = jnp.dot(value, value_hot.T, precision=high)

    combined = neumann_part + jnp.dot(picked, basis[0], precision=high)
    solution = assemble(weights * combined)
    product = jnp.dot(solution.astype(jnp.bfloat16), schur[0], preferred_element_type=jnp.float32)
    residual = force - assemble(4.0 * solution + product)
    return (solution[None], residual[None])


def solution(mesh):
    whole = Mesh(mesh.devices.reshape(SIZES), ALL)
    specs = tuple(P(ALL, *([None] * n)) for n in (2, 2, 2, 2, 1, 1))
    outs = (P(ALL, None, None), P(ALL, None, None))
    return jax.shard_map(local, mesh=whole, in_specs=specs, out_specs=outs, check_vma=False)
```

time: 383 us -> 122 us (0.32)
  the two profiles are of different devices: /device:TPU:248 before, /device:TPU:24 now
where the time goes in v1:
time: 122 us
  blocking collectives  44.1 us (36%)
  waiting for transfers between devices  33.6 us (28%)
  starting transfers between devices  32 us (26%)
  matrix products  5.05 us (4%)
  other arithmetic  3.67 us (3%)
  local copies, waits for them, and re-layouts  2.38 us (2%)
    all_to_all x2, blocking collectives, exchange(): return lax.all_to_all(x, axes, split_axis=0, concat_axis=0, tiled=True)  44.1 us
    all_to_all x2, waiting for transfers between devices, exchange(): return lax.all_to_all(x, axes, split_axis=0, concat_axis=0, tiled=True)  18.7 us
    ppermute x3, waiting for transfers between devices, assemble(): after = lax.ppermute(field[:, :RIM], CHAIN, down)  14.9 us
    all_to_all x2, starting transfers between devices, exchange(): return lax.all_to_all(x, axes, split_axis=0, concat_axis=0, tiled=True)  14.1 us
    ppermute x3, starting transfers between devices, assemble(): before = lax.ppermute(field[:, width - RIM:], CHAIN, up)  10.2 us
    ppermute x3, starting transfers between devices, assemble(): after = lax.ppermute(field[:, :RIM], CHAIN, down)  7.76 us
  transfers between devices with their start and end apart: 8, of which 5 were waited for; matrix products, arithmetic and copies ran while one was open for 2% of the time, Pallas kernels for 0%

profile of v1, /device:TPU:24, one launch (start us, length us, event | category | flops | bytes accessed | tf_op | source)
XLA Modules:
  0.0 121.6 jit_solution(909962103810512620)
XLA Ops:
  0.6 0.0 copy-start
  0.6 0.9 fusion.36
  1.5 3.9 %collective-permute-start = (f32[8,256]{1,0:T(8,128)S(1)}, f32[8,256]{1,0:T(8,128)S(1)}, u32[]{:S(2)}, u32[]{:S(2)}) collective-permute-start(f32[8,256]{1,0:T(8,128)S(1)} %get-tuple-element.14), channel_id=1, source_target_pairs={{0,1},{1,2},{2,3},{3,4},{4,5},{5,6},{6,7},{7,8},{8,9},{9,10},{10,1... | collective-permute-start | bytes 24584 | tf_op jit(solution)/shard_map/ppermute | solution.py:42
  5.4 1.9 %collective-permute-start.1 = (f32[8,256]{1,0:T(8,128)S(1)}, f32[8,256]{1,0:T(8,128)S(1)}, u32[]{:S(2)}, u32[]{:S(2)}) collective-permute-start(f32[8,256]{1,0:T(8,128)S(1)} %get-tuple-element.15), channel_id=1, source_target_pairs={{1,0},{2,1},{3,2},{4,3},{5,4},{6,5},{7,6},{8,7},{9,8},{10,9},{11,1... | collective-permute-start | bytes 24584 | tf_op jit(solution)/shard_map/ppermute | solution.py:43
  7.4 0.7 slice_bitcast_fusion.1
  8.1 0.7 fusion.30
  8.8 0.0 collective-permute-done
  8.8 4.9 %collective-permute-done.1 = f32[8,256]{1,0:T(8,128)S(1)} collective-permute-done((f32[8,256]{1,0:T(8,128)S(1)}, f32[8,256]{1,0:T(8,128)S(1)}, u32[]{:S(2)}, u32[]{:S(2)}) %collective-permute-start.1) | collective-permute-done | bytes 8224 | tf_op jit(solution)/shard_map/ppermute | solution.py:43
  13.7 0.7 slice_add_fusion.3
  14.4 1.1 fusion.13
  15.5 1.0 convolution_bitcast_fusion
  16.4 10.3 %all-to-all-start = ((f32[32,8,128]{2,1,0:T(8,128)}), f32[32,8,128]{2,1,0:T(8,128)S(1)}, u32[]{:S(2)}, u32[]{:S(2)}) async-start(f32[32,8,128]{2,1,0:T(8,128)} %convolution_bitcast_fusion), calls=%async_computation | async-start | bytes 262144 | tf_op jit(solution)/shard_map/all_to_all | solution.py:18
  26.7 0.1 pad.11.clone
  26.8 0.0 copy-start.2
  26.8 7.6 %all-to-all-done = f32[32,8,128]{2,1,0:T(8,128)S(1)} async-done(((f32[32,8,128]{2,1,0:T(8,128)}), f32[32,8,128]{2,1,0:T(8,128)S(1)}, u32[]{:S(2)}, u32[]{:S(2)}) %all-to-all-start) | async-done | bytes 131104 | tf_op jit(solution)/shard_map/all_to_all | solution.py:18
  34.5 0.0 copy-start.1
  34.5 0.9 maximum_maximum_fusion
  35.4 30.0 %all_to_all.20 = f32[24,16,128]{2,1,0:T(8,128)S(1)} all-to-all(f32[24,16,128]{2,1,0:T(8,128)S(1)} %maximum_maximum_fusion), channel_id=1, replica_groups=mesh['yh'=2,'x'=4,'c'=2,'z'=12,'yl'=4] {'z','c'}, dimensions={0} | all-to-all | bytes 393216 | tf_op jit(solution)/shard_map/all_to_all | solution.py:18
  65.4 0.1 fusion.22
  65.6 14.1 %all_to_all.21 = f32[32,8,128]{2,1,0:T(8,128)S(1)} all-to-all(f32[32,8,128]{2,1,0:T(8,128)S(1)} %broadcast_in_dim.29), channel_id=1, replica_groups=mesh['yh'=2,'x'=4,'c'=2,'z'=12,'yl'=4] {'yh','x','yl'}, dimensions={0} | all-to-all | bytes 262144 | tf_op jit(solution)/shard_map/all_to_all | solution.py:18
  79.7 0.6 broadcast_in_dim.30
  80.4 3.8 %all-to-all-start.3 = ((f32[24,8,128]{2,1,0:T(8,128)}), f32[24,8,128]{2,1,0:T(8,128)S(1)}, u32[]{:S(2)}, u32[]{:S(2)}) async-start(f32[24,8,128]{2,1,0:T(8,128)} %broadcast_in_dim.30), calls=%async_computation.3 | async-start | bytes 196608 | tf_op jit(solution)/shard_map/all_to_all | solution.py:18
  84.2 0.0 copy-done
  84.2 0.4 fusion.4
  84.6 11.1 %all-to-all-done.3 = f32[24,8,128]{2,1,0:T(8,128)S(1)} async-done(((f32[24,8,128]{2,1,0:T(8,128)}), f32[24,8,128]{2,1,0:T(8,128)S(1)}, u32[]{:S(2)}, u32[]{:S(2)}) %all-to-all-start.3) | async-done | bytes 98336 | tf_op jit(solution)/shard_map/all_to_all | solution.py:18
  95.7 0.0 copy-done.2
  95.7 0.3 fusion.8
  96.0 0.0 copy-done.1
  96.0 0.2 fusion.7
  96.2 4.3 %collective-permute-start.2 = (f32[8,256]{1,0:T(8,128)S(1)}, f32[8,256]{1,0:T(8,128)S(1)}, u32[]{:S(2)}, u32[]{:S(2)}) collective-permute-start(f32[8,256]{1,0:T(8,128)S(1)} %get-tuple-element.10), channel_id=1, source_target_pairs={{0,1},{1,2},{2,3},{3,4},{4,5},{5,6},{6,7},{7,8},{8,9},{9,10},{10,1... | collective-permute-start | bytes 24584 | tf_op jit(solution)/shard_map/ppermute | solution.py:42
  100.6 1.9 %collective-permute-start.3 = (f32[8,256]{1,0:T(8,128)S(1)}, f32[8,256]{1,0:T(8,128)S(1)}, u32[]{:S(2)}, u32[]{:S(2)}) collective-permute-start(f32[8,256]{1,0:T(8,128)S(1)} %get-tuple-element.11), channel_id=1, source_target_pairs={{1,0},{2,1},{3,2},{4,3},{5,4},{6,5},{7,6},{8,7},{9,8},{10,9},{11,1... | collective-permute-start | bytes 24584 | tf_op jit(solution)/shard_map/ppermute | solution.py:43
  102.5 0.0 collective-permute-done.2
  102.5 6.3 %collective-permute-done.3 = f32[8,256]{1,0:T(8,128)S(1)} collective-permute-done((f32[8,256]{1,0:T(8,128)S(1)}, f32[8,256]{1,0:T(8,128)S(1)}, u32[]{:S(2)}, u32[]{:S(2)}) %collective-permute-start.3) | collective-permute-done | bytes 8224 | tf_op jit(solution)/shard_map/ppermute | solution.py:43
  108.8 2.0 %multiply_add_fusion = f32[8,1024]{1,0:T(8,128)S(1)} fusion(bf16[1,1024,1024]{2,1,0:T(8,128)(2,1)} %param.7, f32[8,256]{1,0:T(8,128)S(1)} %get-tuple-element.9, f32[8,512]{1,0:T(8,128)S(1)} %slice.61, f32[8,256]{1,0:T(8,128)S(1)} %get-tuple-element.8), kind=kOutput, calls=%fused_computation.22 | convolution fusion | flops 16834560 | bytes 2162688 | tf_op jit(solution)/shard_map/dot_general | solution.py:75
  110.8 1.9 %collective-permute-start.4 = (f32[8,256]{1,0:T(8,128)S(1)}, f32[8,256]{1,0:T(8,128)S(1)}, u32[]{:S(2)}, u32[]{:S(2)}) collective-permute-start(f32[8,256]{1,0:T(8,128)S(1)} %get-tuple-element.4), channel_id=1, source_target_pairs={{0,1},{1,2},{2,3},{3,4},{4,5},{5,6},{6,7},{7,8},{8,9},{9,10},{10,1... | collective-permute-start | bytes 24584 | tf_op jit(solution)/shard_map/ppermute | solution.py:42
  112.7 3.9 %collective-permute-start.5 = (f32[8,256]{1,0:T(8,128)S(1)}, f32[8,256]{1,0:T(8,128)S(1)}, u32[]{:S(2)}, u32[]{:S(2)}) collective-permute-start(f32[8,256]{1,0:T(8,128)S(1)} %get-tuple-element.5), channel_id=1, source_target_pairs={{1,0},{2,1},{3,2},{4,3},{5,4},{6,5},{7,6},{8,7},{9,8},{10,9},{11,1... | collective-permute-start | bytes 24584 | tf_op jit(solution)/shard_map/ppermute | solution.py:43
  116.6 0.6 fusion.20
  117.3 0.0 collective-permute-done.4
  117.3 3.7 %collective-permute-done.5 = f32[8,256]{1,0:T(8,128)S(1)} collective-permute-done((f32[8,256]{1,0:T(8,128)S(1)}, f32[8,256]{1,0:T(8,128)S(1)}, u32[]{:S(2)}, u32[]{:S(2)}) %collective-permute-start.5) | collective-permute-done | bytes 8224 | tf_op jit(solution)/shard_map/ppermute | solution.py:43
  121.0 0.6 maximum_subtract_fusion
  (14 shorter events, 0.2 us)
Async XLA Ops:
  0.6 83.6 %copy-start = (bf16[1,1024,1024]{2,1,0:T(8,128)(2,1)S(1)}, bf16[1,1024,1024]{2,1,0:T(8,128)(2,1)}, u32[]{:S(2)}) copy-start(bf16[1,1024,1024]{2,1,0:T(8,128)(2,1)} %param.8) | copy-start | bytes 6291460
  1.5 7.3 %collective-permute-start = (f32[8,256]{1,0:T(8,128)S(1)}, f32[8,256]{1,0:T(8,128)S(1)}, u32[]{:S(2)}, u32[]{:S(2)}) collective-permute-start(f32[8,256]{1,0:T(8,128)S(1)} %get-tuple-element.14), channel_id=1, source_target_pairs={{0,1},{1,2},{2,3},{3,4},{4,5},{5,6},{6,7},{7,8},{8,9},{9,10},{10,1... | collective-permute-start | bytes 24584 | tf_op jit(solution)/shard_map/ppermute | solution.py:42
  5.4 8.3 %collective-permute-start.1 = (f32[8,256]{1,0:T(8,128)S(1)}, f32[8,256]{1,0:T(8,128)S(1)}, u32[]{:S(2)}, u32[]{:S(2)}) collective-permute-start(f32[8,256]{1,0:T(8,128)S(1)} %get-tuple-element.15), channel_id=1, source_target_pairs={{1,0},{2,1},{3,2},{4,3},{5,4},{6,5},{7,6},{8,7},{9,8},{10,9},{11,1... | collective-permute-start | bytes 24584 | tf_op jit(solution)/shard_map/ppermute | solution.py:43
  16.4 18.0 %all-to-all-start = ((f32[32,8,128]{2,1,0:T(8,128)}), f32[32,8,128]{2,1,0:T(8,128)S(1)}, u32[]{:S(2)}, u32[]{:S(2)}) async-start(f32[32,8,128]{2,1,0:T(8,128)} %convolution_bitcast_fusion), calls=%async_computation | async-start | bytes 262144 | tf_op jit(solution)/shard_map/all_to_all | solution.py:18
  26.8 68.9 %copy-start.2 = (s32[1,24]{1,0:T(1,128)S(1)}, s32[1,24]{1,0:T(1,128)}, u32[]{:S(2)}) copy-start(s32[1,24]{1,0:T(1,128)} %param.10) | copy-start | bytes 292
  34.5 61.5 %copy-start.1 = (f32[1,24,1024]{2,1,0:T(8,128)S(1)}, f32[1,24,1024]{2,1,0:T(8,128)}, u32[]{:S(2)}) copy-start(f32[1,24,1024]{2,1,0:T(8,128)} %param.9) | copy-start | bytes 294916
  80.4 15.3 %all-to-all-start.3 = ((f32[24,8,128]{2,1,0:T(8,128)}), f32[24,8,128]{2,1,0:T(8,128)S(1)}, u32[]{:S(2)}, u32[]{:S(2)}) async-start(f32[24,8,128]{2,1,0:T(8,128)} %broadcast_in_dim.30), calls=%async_computation.3 | async-start | bytes 196608 | tf_op jit(solution)/shard_map/all_to_all | solution.py:18
  96.2 6.3 %collective-permute-start.2 = (f32[8,256]{1,0:T(8,128)S(1)}, f32[8,256]{1,0:T(8,128)S(1)}, u32[]{:S(2)}, u32[]{:S(2)}) collective-permute-start(f32[8,256]{1,0:T(8,128)S(1)} %get-tuple-element.10), channel_id=1, source_target_pairs={{0,1},{1,2},{2,3},{3,4},{4,5},{5,6},{6,7},{7,8},{8,9},{9,10},{10,1... | collective-permute-start | bytes 24584 | tf_op jit(solution)/shard_map/ppermute | solution.py:42
  100.6 8.2 %collective-permute-start.3 = (f32[8,256]{1,0:T(8,128)S(1)}, f32[8,256]{1,0:T(8,128)S(1)}, u32[]{:S(2)}, u32[]{:S(2)}) collective-permute-start(f32[8,256]{1,0:T(8,128)S(1)} %get-tuple-element.11), channel_id=1, source_target_pairs={{1,0},{2,1},{3,2},{4,3},{5,4},{6,5},{7,6},{8,7},{9,8},{10,9},{11,1... | collective-permute-start | bytes 24584 | tf_op jit(solution)/shard_map/ppermute | solution.py:43
  110.8 6.5 %collective-permute-start.4 = (f32[8,256]{1,0:T(8,128)S(1)}, f32[8,256]{1,0:T(8,128)S(1)}, u32[]{:S(2)}, u32[]{:S(2)}) collective-permute-start(f32[8,256]{1,0:T(8,128)S(1)} %get-tuple-element.4), channel_id=1, source_target_pairs={{0,1},{1,2},{2,3},{3,4},{4,5},{5,6},{6,7},{7,8},{8,9},{9,10},{10,1... | collective-permute-start | bytes 24584 | tf_op jit(solution)/shard_map/ppermute | solution.py:42
  112.7 8.2 %collective-permute-start.5 = (f32[8,256]{1,0:T(8,128)S(1)}, f32[8,256]{1,0:T(8,128)S(1)}, u32[]{:S(2)}, u32[]{:S(2)}) collective-permute-start(f32[8,256]{1,0:T(8,128)S(1)} %get-tuple-element.5), channel_id=1, source_target_pairs={{1,0},{2,1},{3,2},{4,3},{5,4},{6,5},{7,6},{8,7},{9,8},{10,9},{11,1... | collective-permute-start | bytes 24584 | tf_op jit(solution)/shard_map/ppermute | solution.py:43

commit v2 on v1

v2 whole, which is shorter than its diff:
```python
import jax
import jax.numpy as jnp
from jax import lax
from jax.experimental import pallas as pl
from jax.experimental.pallas import tpu as pltpu
from jax.sharding import Mesh, PartitionSpec as P


RIM = 256
ALL = ("yh", "x", "c", "z", "yl")
SIZES = (2, 4, 2, 12, 4)
CHAIN = ("z", "yl")
ROWS = ("yh", "x", "yl")
COLS = ("z", "c")
CHAIN_LENGTH = 48
N_ROWS = 32
N_COLS = 24
SLOT_BEFORE = 32
SLOT_AFTER = 64
LANES = 128
HIGH = lax.Precision.HIGHEST
F32 = jnp.float32
BF16 = jnp.bfloat16


def exchange(x, axes):
    return lax.all_to_all(x, axes, split_axis=0, concat_axis=0, tiled=True)


def position_of(index):
    owner = index // 4
    group, member = owner // 48, owner % 48
    row_part = (group // 2) * 4 + member % 4
    col_part = (member // 4) * 2 + group % 2
    return row_part * LANES + col_part * 4 + index % 4


def three_parts(x):
    first = x.astype(BF16)
    rest = x - first.astype(F32)
    second = rest.astype(BF16)
    third = (rest - second.astype(F32)).astype(BF16)
    return jnp.concatenate([first.astype(F32), second.astype(F32), third.astype(F32)], axis=0).astype(BF16)


def added(x):
    return x[0:8] + x[8:16] + x[16:24]


def scatter_kernel(lower, middle, upper, before, after, scaled_basis, place, force, out):
    whole = jnp.concatenate([lower[...] + before[...], middle[...], upper[...] + after[...]], axis=1)
    force[...] = whole
    terms = lax.dot_general(whole, scaled_basis[...], (((1,), (1,)), ((), ())), precision=HIGH, preferred_element_type=F32)
    columns = lax.broadcasted_iota(jnp.int32, (place.shape[0], N_ROWS * LANES), 1)
    hot = (columns == place[...]).astype(F32).astype(BF16)
    dense = added(jnp.dot(three_parts(terms), hot, preferred_element_type=F32))
    for p in range(N_ROWS):
        out[p] = dense[:, p * LANES : (p + 1) * LANES]


def spread_kernel(arrived, out):
    total = jnp.sum(arrived[...], axis=0)
    out[...] = jnp.broadcast_to(total[None], out.shape)


def block_kernel(arrived, block, out):
    total = jnp.sum(arrived[...], axis=0)[:, : block.shape[0]]
    value = jnp.dot(total, block[...], precision=HIGH, preferred_element_type=F32)
    out[...] = jnp.broadcast_to(value[None], out.shape)


def finish_kernel(value, names, scaled_basis, neumann_part, before, after, schur, solution, applied, held, sems):
    width = neumann_part.shape[1]
    cases, corners = neumann_part.shape[0], scaled_basis.shape[0]
    copies = [
        pltpu.make_async_copy(schur.at[pl.ds(k * RIM, RIM)], held.at[pl.ds(k * RIM, RIM)], sems.at[k])
        for k in range(width // RIM)
    ]
    for copy in copies:
        copy.start()
    last = cases + corners
    wanted = names[...] + before[last : last + 1, :LANES] + after[last : last + 1, :LANES]
    found = jnp.zeros((3 * cases, LANES), F32)
    for q in range(N_COLS):
        rows = lax.broadcasted_iota(jnp.int32, (LANES, LANES), 0) + (q * LANES + 1)
        hot = (rows.astype(F32) == wanted).astype(F32).astype(BF16)
        found += jnp.dot(three_parts(value[q]), hot, preferred_element_type=F32)
    picked = added(found)

    def coarse(slot, basis):
        return jnp.dot(picked[:, slot : slot + corners], basis, precision=HIGH, preferred_element_type=F32)

    u = neumann_part[...] + coarse(0, scaled_basis[...])
    lower = u[:, :RIM] + before[:cases] + coarse(SLOT_BEFORE, before[cases:last])
    upper = u[:, width - RIM :] + after[:cases] + coarse(SLOT_AFTER, after[cases:last])
    u = jnp.concatenate([lower, u[:, RIM : width - RIM], upper], axis=1)
    solution[...] = u
    total = 4.0 * u
    rounded = u.astype(BF16)
    for k, copy in enumerate(copies):
        copy.wait()
        part = rounded[:, k * RIM : (k + 1) * RIM]
        total += jnp.dot(part, held[k * RIM : (k + 1) * RIM], preferred_element_type=F32)
    applied[...] = total


def call(kernel, shapes, *args, in_hbm=(), scratch=(), limit=24 << 20):
    shapes = [jax.ShapeDtypeStruct(s, F32) for s in shapes]
    return pl.pallas_call(
        kernel,
        out_shape=shapes,
        in_specs=[pl.BlockSpec(memory_space=pltpu.HBM if i in in_hbm else pltpu.VMEM) for i in range(len(args))],
        out_specs=[pl.BlockSpec(memory_space=pltpu.VMEM)] * len(shapes),
        scratch_shapes=list(scratch),
        compiler_params=pltpu.CompilerParams(vmem_limit_bytes=limit),
    )(*args)


def local(loads, schur, neumann, basis, coarse_index, coarse_inverse):
    loads, schur, neumann, basis, index = loads[0], schur[0], neumann[0], basis[0], coarse_index[0]
    cases, width = loads.shape
    corners = basis.shape[0]
    position = lax.axis_index(CHAIN)
    columns = lax.broadcasted_iota(jnp.int32, (1, width), 1)
    lower_rim = (columns < RIM) & (position > 0)
    upper_rim = (columns >= width - RIM) & (position < CHAIN_LENGTH - 1)
    weights = jnp.where(lower_rim | upper_rim, 0.5, 1.0).astype(F32)
    up = [(i, i + 1) for i in range(CHAIN_LENGTH - 1)]
    down = [(j, i) for i, j in up]

    def rims(field):
        before = lax.ppermute(field[:, width - RIM :], CHAIN, up)
        after = lax.ppermute(field[:, :RIM], CHAIN, down)
        return before, after

    def assemble(field):
        before, after = rims(field)
        middle = field[:, RIM : width - RIM]
        return jnp.concatenate([field[:, :RIM] + before, middle, field[:, width - RIM :] + after], axis=1)

    lower, middle, upper = loads[:, :RIM], loads[:, RIM : width - RIM], loads[:, width - RIM :]
    before = lax.ppermute(upper, CHAIN, up)
    after = lax.ppermute(lower, CHAIN, down)
    block = exchange(coarse_inverse.reshape(4, N_COLS, LANES).transpose(1, 0, 2), COLS).reshape(4 * N_COLS, LANES)
    place = position_of(index)[:, None]
    scaled_basis = weights * basis
    force, partial = call(
        scatter_kernel, [(cases, width), (N_ROWS, cases, LANES)], lower, middle, upper, before, after, scaled_basis, place
    )
    partial, block = lax.optimization_barrier((partial, block))
    arrived = exchange(partial, ROWS)

    weighted = weights * force
    product = jnp.dot(weighted.astype(BF16), neumann, preferred_element_type=F32)
    neumann_part = weights * (0.25 * weighted + 0.0625 * product)
    named = index.astype(F32)[None] + 1.0

    def names(slot, rows, size):
        return jnp.pad(named, ((0, rows - 1), (slot, size - slot - corners)))

    to_next = jnp.concatenate(
        [neumann_part[:, width - RIM :], scaled_basis[:, width - RIM :], names(SLOT_BEFORE, 8, RIM)], axis=0
    )
    to_last = jnp.concatenate([neumann_part[:, :RIM], scaled_basis[:, :RIM], names(SLOT_AFTER, 8, RIM)], axis=0)
    own_names = names(0, 1, LANES)
    told_before = lax.ppermute(to_next, CHAIN, up)
    told_after = lax.ppermute(to_last, CHAIN, down)

    (sent,) = call(spread_kernel, [(N_COLS, cases, LANES)], arrived)
    arrived = exchange(sent, COLS)
    arrived, own_names = lax.optimization_barrier((arrived, own_names))
    (sent,) = call(block_kernel, [(N_ROWS, cases, LANES)], arrived, block)
    arrived = exchange(sent, ROWS)
    (sent,) = call(spread_kernel, [(N_COLS, cases, LANES)], arrived)
    value = exchange(sent, COLS)
    u, applied = call(
        finish_kernel, [(cases, width), (cases, width)],
        value, own_names, scaled_basis, neumann_part, told_before, told_after, schur,
        in_hbm=(6,), limit=60 * 1024 * 1024, scratch=(pltpu.VMEM(schur.shape, BF16), pltpu.SemaphoreType.DMA((width // RIM,))),
    )
    residual = force - assemble(applied)
    return (u[None], residual[None])


def solution(mesh):
    whole = Mesh(mesh.devices.reshape(SIZES), ALL)
    specs = tuple(P(ALL, *([None] * n)) for n in (2, 2, 2, 2, 1, 1))
    outs = (P(ALL, None, None), P(ALL, None, None))
    return jax.shard_map(local, mesh=whole, in_specs=specs, out_specs=outs, check_vma=False)
```

time: 122 us -> 123 us (level)
  the two profiles are of different devices: /device:TPU:24 before, /device:TPU:216 now
where the time goes in v2:
time: 123 us; the launch traced here: 122 us
  starting transfers between devices  53 us (43%)
  waiting for transfers between devices  33.3 us (27%)
  blocking collectives  20.6 us (17%)
  Pallas kernels  6 us (5%)
  local copies, waits for them, and re-layouts  5.01 us (4%)
  other arithmetic  3.04 us (2%)
    all_to_all x4, starting transfers between devices, exchange(): return lax.all_to_all(x, axes, split_axis=0, concat_axis=0, tiled=True)  30.9 us
    all_to_all x4, waiting for transfers between devices, exchange(): return lax.all_to_all(x, axes, split_axis=0, concat_axis=0, tiled=True)  20.6 us
    all_to_all x1, blocking collectives, exchange(): return lax.all_to_all(x, axes, split_axis=0, concat_axis=0, tiled=True)  20.6 us
    ppermute x1, waiting for transfers between devices, local(): told_after = lax.ppermute(to_last, CHAIN, down)  7.85 us
    ppermute x1, starting transfers between devices, local(): told_before = lax.ppermute(to_next, CHAIN, up)  7.3 us
    pallas_call x5, Pallas kernels, call(): pl.pallas_call(kernel, out_shape=shapes, in_specs=[pl.BlockSpec(memory_sp...  6 us
    ppermute x1, starting transfers between devices, local(): before = lax.ppermute(upper, CHAIN, up)  5.14 us
    ppermute x1, waiting for transfers between devices, rims(): after = lax.ppermute(field[:, :RIM], CHAIN, down)  4.8 us
  transfers between devices with their start and end apart: 10, of which 5 were waited for; matrix products, arithmetic and copies ran while one was open for 4% of the time, Pallas kernels for 0%

profile of v2, /device:TPU:216, one launch (start us, length us, event | category | flops | bytes accessed | tf_op | source)
XLA Modules:
  0.0 122.1 jit_solution(12469921600374687765)
XLA Ops:
  0.6 0.0 copy-start
  0.6 0.9 fusion.34
  1.5 5.1 %collective-permute-start = (f32[8,256]{1,0:T(8,128)S(1)}, f32[8,256]{1,0:T(8,128)S(1)}, u32[]{:S(2)}, u32[]{:S(2)}) collective-permute-start(f32[8,256]{1,0:T(8,128)S(1)} %get-tuple-element.26.upper), channel_id=1, source_target_pairs={{0,1},{1,2},{2,3},{3,4},{4,5},{5,6},{6,7},{7,8},{8,9},{9,10},{10,1... | collective-permute-start | bytes 24584 | tf_op jit(solution)/shard_map/ppermute | solution.py:142
  6.7 1.9 %collective-permute-start.1 = (f32[8,256]{1,0:T(8,128)S(1)}, f32[8,256]{1,0:T(8,128)S(1)}, u32[]{:S(2)}, u32[]{:S(2)}) collective-permute-start(f32[8,256]{1,0:T(8,128)S(1)} %get-tuple-element.27.lower), channel_id=1, source_target_pairs={{1,0},{2,1},{3,2},{4,3},{5,4},{6,5},{7,6},{8,7},{9,8},{10,9},{11,1... | collective-permute-start | bytes 24584 | tf_op jit(solution)/shard_map/ppermute | solution.py:143
  8.6 11.8 %all-to-all-start = ((f32[24,4,128]{2,1,0:T(4,128)}), f32[24,4,128]{2,1,0:T(4,128)S(1)}, u32[]{:S(2)}, u32[]{:S(2)}) async-start(f32[24,4,128]{2,1,0:T(4,128)} %bitcast.21), calls=%async_computation | async-start | bytes 98304 | tf_op jit(solution)/shard_map/all_to_all | solution.py:27
  20.4 0.7 copy.8
  21.2 0.9 bitcast_multiply_fusion.scaled_basis
  22.1 0.0 copy-start.1
  22.1 0.1 fusion.13.place
  22.1 0.7 slice.43.middle
  22.9 0.0 collective-permute-done.before
  22.9 0.0 collective-permute-done.1.after
  22.9 0.5 shard_map.77
  23.4 4.7 %all-to-all-done = f32[24,4,128]{2,1,0:T(4,128)S(1)} async-done(((f32[24,4,128]{2,1,0:T(4,128)}), f32[24,4,128]{2,1,0:T(4,128)S(1)}, u32[]{:S(2)}, u32[]{:S(2)}) %all-to-all-start) | async-done | bytes 49184 | tf_op jit(solution)/shard_map/all_to_all | solution.py:27
  28.1 20.6 %all_to_all.25.arrived = f32[32,8,128]{2,1,0:T(8,128)S(1)} all-to-all(f32[32,8,128]{2,1,0:T(8,128)S(1)} %get-tuple-element.11), channel_id=1, replica_groups=mesh['yh'=2,'x'=4,'c'=2,'z'=12,'yl'=4] {'yh','x','yl'}, dimensions={0} | all-to-all | bytes 262144 | tf_op jit(solution)/shard_map/all_to_all | solution.py:27
  48.6 0.7 shard_map.78
  49.3 6.4 %all-to-all-start.2 = ((f32[24,8,128]{2,1,0:T(8,128)}), f32[24,8,128]{2,1,0:T(8,128)S(1)}, u32[]{:S(2)}, u32[]{:S(2)}) async-start(f32[24,8,128]{2,1,0:T(8,128)} %shard_map.78), calls=%async_computation.2 | async-start | bytes 196608 | tf_op jit(solution)/shard_map/all_to_all | solution.py:27
  55.8 0.7 convert_add_fusion
  56.4 0.6 pad.12.names
  57.0 7.6 %all-to-all-done.2.arrived = f32[24,8,128]{2,1,0:T(8,128)S(1)} async-done(((f32[24,8,128]{2,1,0:T(8,128)}), f32[24,8,128]{2,1,0:T(8,128)S(1)}, u32[]{:S(2)}, u32[]{:S(2)}) %all-to-all-start.2) | async-done | bytes 98336 | tf_op jit(solution)/shard_map/all_to_all | solution.py:27
  64.6 0.8 shard_map.79
  65.4 6.7 %all-to-all-start.3 = ((f32[32,8,128]{2,1,0:T(8,128)}), f32[32,8,128]{2,1,0:T(8,128)S(1)}, u32[]{:S(2)}, u32[]{:S(2)}) async-start(f32[32,8,128]{2,1,0:T(8,128)} %shard_map.79), calls=%async_computation.3 | async-start | bytes 262144 | tf_op jit(solution)/shard_map/all_to_all | solution.py:27
  72.1 0.0 copy-done
  72.2 0.4 add_multiply_fusion.neumann_part
  72.5 8.4 %all-to-all-done.3.arrived = f32[32,8,128]{2,1,0:T(8,128)S(1)} async-done(((f32[32,8,128]{2,1,0:T(8,128)}), f32[32,8,128]{2,1,0:T(8,128)S(1)}, u32[]{:S(2)}, u32[]{:S(2)}) %all-to-all-start.3) | async-done | bytes 131104 | tf_op jit(solution)/shard_map/all_to_all | solution.py:27
  80.9 0.7 shard_map.80
  81.6 5.9 %all-to-all-start.4 = ((f32[24,8,128]{2,1,0:T(8,128)}), f32[24,8,128]{2,1,0:T(8,128)S(1)}, u32[]{:S(2)}, u32[]{:S(2)}) async-start(f32[24,8,128]{2,1,0:T(8,128)} %shard_map.80), calls=%async_computation.4 | async-start | bytes 196608 | tf_op jit(solution)/shard_map/all_to_all | solution.py:27
  87.5 0.1 select_maximum_fusion
  87.6 0.0 copy-done.1
  87.6 7.3 %collective-permute-start.2 = (f32[40,256]{1,0:T(8,128)S(1)}, f32[40,256]{1,0:T(8,128)S(1)}, u32[]{:S(2)}, u32[]{:S(2)}) collective-permute-start(f32[40,256]{1,0:T(8,128)S(1)} %get-tuple-element.29), channel_id=1, source_target_pairs={{0,1},{1,2},{2,3},{3,4},{4,5},{5,6},{6,7},{7,8},{8,9},{9,10},{10,1... | collective-permute-start | bytes 122888 | tf_op jit(solution)/shard_map/ppermute | solution.py:166
  94.9 1.9 %collective-permute-start.3 = (f32[40,256]{1,0:T(8,128)S(1)}, f32[40,256]{1,0:T(8,128)S(1)}, u32[]{:S(2)}, u32[]{:S(2)}) collective-permute-start(f32[40,256]{1,0:T(8,128)S(1)} %get-tuple-element.28), channel_id=1, source_target_pairs={{1,0},{2,1},{3,2},{4,3},{5,4},{6,5},{7,6},{8,7},{9,8},{10,9},{11,1... | collective-permute-start | bytes 122888 | tf_op jit(solution)/shard_map/ppermute | solution.py:167
  96.8 0.0 collective-permute-done.2.before
  96.8 0.0 copy-start.4
  96.8 7.9 %collective-permute-done.3.after = f32[40,256]{1,0:T(8,128)S(1)} collective-permute-done((f32[40,256]{1,0:T(8,128)S(1)}, f32[40,256]{1,0:T(8,128)S(1)}, u32[]{:S(2)}, u32[]{:S(2)}) %collective-permute-start.3) | collective-permute-done | bytes 40992 | tf_op jit(solution)/shard_map/ppermute | solution.py:167
  104.7 0.0 all-to-all-done.4.value
  104.7 0.0 copy-done.3
  104.7 0.0 copy-done.4
  104.7 0.6 copy-done.5
  105.3 0.0 copy-done.2
  105.3 3.3 %shard_map.81 = (f32[8,1024]{1,0:T(8,128)}, f32[8,1024]{1,0:T(8,128)}) custom-call(f32[24,8,128]{2,1,0:T(8,128)} %copy-done.2, f32[1,128]{1,0:T(1,128)} %pad.12.names, f32[24,1024]{1,0:T(8,128)} %copy-done.1, f32[8,1024]{1,0:T(8,128)} %copy-done.3, f32[40,256]{1,0:T(8,128)} %copy-done.4, f32[40,256]{1,0:T(8,128)} %copy-done.5, bf16[1024,1024]{1,0:T(8,128)(2,1)} %bitcast.20), custom_call_target="tpu_custom_call" | custom-call | tf_op jit(solution)/shard_map/pallas_call | solution.py:109
  108.7 0.7 fusion.32
  109.4 1.9 %collective-permute-start.4 = (f32[8,256]{1,0:T(8,128)S(1)}, f32[8,256]{1,0:T(8,128)S(1)}, u32[]{:S(2)}, u32[]{:S(2)}) collective-permute-start(f32[8,256]{1,0:T(8,128)S(1)} %get-tuple-element.22), channel_id=1, source_target_pairs={{0,1},{1,2},{2,3},{3,4},{4,5},{5,6},{6,7},{7,8},{8,9},{9,10},{10,1... | collective-permute-start | bytes 24584 | tf_op jit(solution)/shard_map/ppermute | solution.py:132
  111.3 3.9 %collective-permute-start.5 = (f32[8,256]{1,0:T(8,128)S(1)}, f32[8,256]{1,0:T(8,128)S(1)}, u32[]{:S(2)}, u32[]{:S(2)}) collective-permute-start(f32[8,256]{1,0:T(8,128)S(1)} %get-tuple-element.23), channel_id=1, source_target_pairs={{1,0},{2,1},{3,2},{4,3},{5,4},{6,5},{7,6},{8,7},{9,8},{10,9},{11,1... | collective-permute-start | bytes 24584 | tf_op jit(solution)/shard_map/ppermute | solution.py:133
  115.2 0.7 slice.41
  115.9 0.0 collective-permute-done.4
  115.9 4.8 %collective-permute-done.5 = f32[8,256]{1,0:T(8,128)S(1)} collective-permute-done((f32[8,256]{1,0:T(8,128)S(1)}, f32[8,256]{1,0:T(8,128)S(1)}, u32[]{:S(2)}, u32[]{:S(2)}) %collective-permute-start.5) | collective-permute-done | bytes 8224 | tf_op jit(solution)/shard_map/ppermute | solution.py:133
  120.7 0.7 slice_add_fusion.1
  121.5 0.6 fusion.5
  (6 shorter events, 0.0 us)
Async XLA Ops:
  0.6 71.5 %copy-start = (bf16[1,1024,1024]{2,1,0:T(8,128)(2,1)S(1)}, bf16[1,1024,1024]{2,1,0:T(8,128)(2,1)}, u32[]{:S(2)}) copy-start(bf16[1,1024,1024]{2,1,0:T(8,128)(2,1)} %param.8) | copy-start | bytes 6291460
  1.5 21.4 %collective-permute-start = (f32[8,256]{1,0:T(8,128)S(1)}, f32[8,256]{1,0:T(8,128)S(1)}, u32[]{:S(2)}, u32[]{:S(2)}) collective-permute-start(f32[8,256]{1,0:T(8,128)S(1)} %get-tuple-element.26.upper), channel_id=1, source_target_pairs={{0,1},{1,2},{2,3},{3,4},{4,5},{5,6},{6,7},{7,8},{8,9},{9,10},{10,1... | collective-permute-start | bytes 24584 | tf_op jit(solution)/shard_map/ppermute | solution.py:142
  6.7 16.2 %collective-permute-start.1 = (f32[8,256]{1,0:T(8,128)S(1)}, f32[8,256]{1,0:T(8,128)S(1)}, u32[]{:S(2)}, u32[]{:S(2)}) collective-permute-start(f32[8,256]{1,0:T(8,128)S(1)} %get-tuple-element.27.lower), channel_id=1, source_target_pairs={{1,0},{2,1},{3,2},{4,3},{5,4},{6,5},{7,6},{8,7},{9,8},{10,9},{11,1... | collective-permute-start | bytes 24584 | tf_op jit(solution)/shard_map/ppermute | solution.py:143
  8.6 19.5 %all-to-all-start = ((f32[24,4,128]{2,1,0:T(4,128)}), f32[24,4,128]{2,1,0:T(4,128)S(1)}, u32[]{:S(2)}, u32[]{:S(2)}) async-start(f32[24,4,128]{2,1,0:T(4,128)} %bitcast.21), calls=%async_computation | async-start | bytes 98304 | tf_op jit(solution)/shard_map/all_to_all | solution.py:27
  22.1 65.5 %copy-start.1 = (f32[24,1024]{1,0:T(8,128)}, f32[24,1024]{1,0:T(8,128)S(1)}, u32[]{:S(2)}) copy-start(f32[24,1024]{1,0:T(8,128)S(1)} %bitcast_multiply_fusion.scaled_basis) | copy-start | bytes 294916
  49.3 15.3 %all-to-all-start.2 = ((f32[24,8,128]{2,1,0:T(8,128)}), f32[24,8,128]{2,1,0:T(8,128)S(1)}, u32[]{:S(2)}, u32[]{:S(2)}) async-start(f32[24,8,128]{2,1,0:T(8,128)} %shard_map.78), calls=%async_computation.2 | async-start | bytes 196608 | tf_op jit(solution)/shard_map/all_to_all | solution.py:27
  65.4 15.5 %all-to-all-start.3 = ((f32[32,8,128]{2,1,0:T(8,128)}), f32[32,8,128]{2,1,0:T(8,128)S(1)}, u32[]{:S(2)}, u32[]{:S(2)}) async-start(f32[32,8,128]{2,1,0:T(8,128)} %shard_map.79), calls=%async_computation.3 | async-start | bytes 262144 | tf_op jit(solution)/shard_map/all_to_all | solution.py:27
  72.5 32.1 %copy-start.3 = (f32[8,1024]{1,0:T(8,128)}, f32[8,1024]{1,0:T(8,128)S(1)}, u32[]{:S(2)}) copy-start(f32[8,1024]{1,0:T(8,128)S(1)} %add_multiply_fusion.neumann_part) | copy-start | bytes 98308
  81.6 23.1 %all-to-all-start.4 = ((f32[24,8,128]{2,1,0:T(8,128)}), f32[24,8,128]{2,1,0:T(8,128)S(1)}, u32[]{:S(2)}, u32[]{:S(2)}) async-start(f32[24,8,128]{2,1,0:T(8,128)} %shard_map.80), calls=%async_computation.4 | async-start | bytes 196608 | tf_op jit(solution)/shard_map/all_to_all | solution.py:27
  87.6 9.2 %collective-permute-start.2 = (f32[40,256]{1,0:T(8,128)S(1)}, f32[40,256]{1,0:T(8,128)S(1)}, u32[]{:S(2)}, u32[]{:S(2)}) collective-permute-start(f32[40,256]{1,0:T(8,128)S(1)} %get-tuple-element.29), channel_id=1, source_target_pairs={{0,1},{1,2},{2,3},{3,4},{4,5},{5,6},{6,7},{7,8},{8,9},{9,10},{10,1... | collective-permute-start | bytes 122888 | tf_op jit(solution)/shard_map/ppermute | solution.py:166
  94.9 9.8 %collective-permute-start.3 = (f32[40,256]{1,0:T(8,128)S(1)}, f32[40,256]{1,0:T(8,128)S(1)}, u32[]{:S(2)}, u32[]{:S(2)}) collective-permute-start(f32[40,256]{1,0:T(8,128)S(1)} %get-tuple-element.28), channel_id=1, source_target_pairs={{1,0},{2,1},{3,2},{4,3},{5,4},{6,5},{7,6},{8,7},{9,8},{10,9},{11,1... | collective-permute-start | bytes 122888 | tf_op jit(solution)/shard_map/ppermute | solution.py:167
  96.8 7.9 %copy-start.4 = (f32[40,256]{1,0:T(8,128)}, f32[40,256]{1,0:T(8,128)S(1)}, u32[]{:S(2)}) copy-start(f32[40,256]{1,0:T(8,128)S(1)} %collective-permute-done.2.before) | copy-start | bytes 122884
  104.7 0.6 copy-start.5
  104.7 0.7 copy-start.2
  109.4 6.6 %collective-permute-start.4 = (f32[8,256]{1,0:T(8,128)S(1)}, f32[8,256]{1,0:T(8,128)S(1)}, u32[]{:S(2)}, u32[]{:S(2)}) collective-permute-start(f32[8,256]{1,0:T(8,128)S(1)} %get-tuple-element.22), channel_id=1, source_target_pairs={{0,1},{1,2},{2,3},{3,4},{4,5},{5,6},{6,7},{7,8},{8,9},{9,10},{10,1... | collective-permute-start | bytes 24584 | tf_op jit(solution)/shard_map/ppermute | solution.py:132
  111.3 9.5 %collective-permute-start.5 = (f32[8,256]{1,0:T(8,128)S(1)}, f32[8,256]{1,0:T(8,128)S(1)}, u32[]{:S(2)}, u32[]{:S(2)}) collective-permute-start(f32[8,256]{1,0:T(8,128)S(1)} %get-tuple-element.23), channel_id=1, source_target_pairs={{1,0},{2,1},{3,2},{4,3},{5,4},{6,5},{7,6},{8,7},{9,8},{10,9},{11,1... | collective-permute-start | bytes 24584 | tf_op jit(solution)/shard_map/ppermute | solution.py:133

commit v3 on v2

--- a/solution.py
+++ b/solution.py
@@ -17,6 +17,7 @@
 N_COLS = 24
 SLOT_BEFORE = 32
 SLOT_AFTER = 64
+LIMIT = 53 << 20
 LANES = 128
 HIGH = lax.Precision.HIGHEST
 F32 = jnp.float32
@@ -45,6 +46,29 @@
 
 def added(x):
     return x[0:8] + x[8:16] + x[16:24]
+
+
+def prepare_kernel(basis, weights, index, inverse, scaled, place, names, up_basis, down_basis, blocks):
+    width, corners = basis.shape[1], basis.shape[0]
+    shared = weights[...] * basis[...]
+    scaled[...] = shared
+    square = (corners, corners)
+    same = lax.broadcasted_iota(jnp.int32, square, 0) == lax.broadcasted_iota(jnp.int32, square, 1)
+    column = jnp.sum(jnp.where(same, index[...].astype(F32), 0.0), axis=1, keepdims=True).astype(jnp.int32)
+    place[...] = position_of(column)
+    named = index[...].astype(F32) + 1.0
+    gap = jnp.zeros((1, SLOT_BEFORE - corners), F32)
+    row = jnp.concatenate([named, gap, named, gap, named, gap, jnp.zeros((1, SLOT_BEFORE), F32)], axis=1)
+    lanes = lax.broadcasted_iota(jnp.int32, (1, LANES), 1)
+    names[...] = jnp.where(lanes < corners, row, 0.0)
+    first = lax.broadcasted_iota(jnp.int32, (8, LANES), 0) == 0
+    for slot, out, rim in ((SLOT_BEFORE, up_basis, shared[:, width - RIM :]), (SLOT_AFTER, down_basis, shared[:, :RIM])):
+        out[:corners] = rim
+        mine = first & (lanes >= slot) & (lanes < slot + corners)
+        told = jnp.where(mine, jnp.broadcast_to(row, (8, LANES)), 0.0)
+        out[corners:] = jnp.concatenate([told, jnp.zeros((8, RIM - LANES), F32)], axis=1)
+    for q in range(N_COLS):
+        blocks[q] = inverse[:, q * LANES : (q + 1) * LANES]
 
 
 def scatter_kernel(lower, middle, upper, before, after, scaled_basis, place, force, out):
@@ -63,9 +87,19 @@
     out[...] = jnp.broadcast_to(total[None], out.shape)
 
 
-def block_kernel(arrived, block, out):
-    total = jnp.sum(arrived[...], axis=0)[:, : block.shape[0]]
-    value = jnp.dot(total, block[...], precision=HIGH, preferred_element_type=F32)
+def spread_with_blocks_kernel(arrived, blocks, out):
+    total = jnp.sum(arrived[...], axis=0)
+    for q in range(N_COLS):
+        out[q, 0] = total[0:4]
+        out[q, 1] = total[4:8]
+        out[q, 2] = blocks[q]
+
+
+def block_kernel(arrived, out, block):
+    total = jnp.concatenate([jnp.sum(arrived[:, 0], axis=0), jnp.sum(arrived[:, 1], axis=0)], axis=0)
+    for q in range(N_COLS):
+        block[4 * q : 4 * q + 4] = arrived[q, 2]
+    value = jnp.dot(total[:, : block.shape[0]], block[...], precision=HIGH, preferred_element_type=F32)
     out[...] = jnp.broadcast_to(value[None], out.shape)
 
 
@@ -105,7 +139,7 @@
 
 
 def call(kernel, shapes, *args, in_hbm=(), scratch=(), limit=24 << 20):
-    shapes = [jax.ShapeDtypeStruct(s, F32) for s in shapes]
+    shapes = [s if isinstance(s, jax.ShapeDtypeStruct) else jax.ShapeDtypeStruct(s, F32) for s in shapes]
     return pl.pallas_call(
         kernel,
         out_shape=shapes,
@@ -141,42 +175,42 @@
     lower, middle, upper = loads[:, :RIM], loads[:, RIM : width - RIM], loads[:, width - RIM :]
     before = lax.ppermute(upper, CHAIN, up)
     after = lax.ppermute(lower, CHAIN, down)
-    block = exchange(coarse_inverse.reshape(4, N_COLS, LANES).transpose(1, 0, 2), COLS).reshape(4 * N_COLS, LANES)
-    place = position_of(index)[:, None]
-    scaled_basis = weights * basis
+    own = corners + 8
+    scaled_basis, place, own_names, up_basis, down_basis, blocks = call(
+        prepare_kernel,
+        [
+            (corners, width), jax.ShapeDtypeStruct((corners, 1), jnp.int32), (1, LANES),
+            (own, RIM), (own, RIM), (N_COLS, 4, LANES),
+        ],
+        basis, weights, index[None], coarse_inverse,
+    )
     force, partial = call(
         scatter_kernel, [(cases, width), (N_ROWS, cases, LANES)], lower, middle, upper, before, after, scaled_basis, place
     )
-    partial, block = lax.optimization_barrier((partial, block))
     arrived = exchange(partial, ROWS)
+    (sent,) = call(spread_with_blocks_kernel, [(N_COLS, 3, 4, LANES)], arrived, blocks)
+    force, sent, weights = lax.optimization_barrier((force, sent, weights))
 
     weighted = weights * force
     product = jnp.dot(weighted.astype(BF16), neumann, preferred_element_type=F32)
     neumann_part = weights * (0.25 * weighted + 0.0625 * product)
-    named = index.astype(F32)[None] + 1.0
-
-    def names(slot, rows, size):
-        return jnp.pad(named, ((0, rows - 1), (slot, size - slot - corners)))
-
-    to_next = jnp.concatenate(
-        [neumann_part[:, width - RIM :], scaled_basis[:, width - RIM :], names(SLOT_BEFORE, 8, RIM)], axis=0
-    )
-    to_last = jnp.concatenate([neumann_part[:, :RIM], scaled_basis[:, :RIM], names(SLOT_AFTER, 8, RIM)], axis=0)
-    own_names = names(0, 1, LANES)
+    to_next = jnp.concatenate([neumann_part[:, width - RIM :], up_basis], axis=0)
+    to_last = jnp.concatenate([neumann_part[:, :RIM], down_basis], axis=0)
     told_before = lax.ppermute(to_next, CHAIN, up)
     told_after = lax.ppermute(to_last, CHAIN, down)
 
-    (sent,) = call(spread_kernel, [(N_COLS, cases, LANES)], arrived)
     arrived = exchange(sent, COLS)
-    arrived, own_names = lax.optimization_barrier((arrived, own_names))
-    (sent,) = call(block_kernel, [(N_ROWS, cases, LANES)], arrived, block)
+    arrived, told_before, told_after = lax.optimization_barrier((arrived, told_before, told_after))
+    (sent,) = call(
+        block_kernel, [(N_ROWS, cases, LANES)], arrived, scratch=(pltpu.VMEM((4 * N_COLS, LANES), F32),)
+    )
     arrived = exchange(sent, ROWS)
     (sent,) = call(spread_kernel, [(N_COLS, cases, LANES)], arrived)
     value = exchange(sent, COLS)
     u, applied = call(
         finish_kernel, [(cases, width), (cases, width)],
         value, own_names, scaled_basis, neumann_part, told_before, told_after, schur,
-        in_hbm=(6,), limit=60 * 1024 * 1024, scratch=(pltpu.VMEM(schur.shape, BF16), pltpu.SemaphoreType.DMA((width // RIM,))),
+        in_hbm=(6,), limit=LIMIT, scratch=(pltpu.VMEM(schur.shape, BF16), pltpu.SemaphoreType.DMA((width // RIM,))),
     )
     residual = force - assemble(applied)
     return (u[None], residual[None])

time: 123 us -> 114 us (0.927)
  the two profiles are of different devices: /device:TPU:216 before, /device:TPU:24 now
where the time goes in v3:
time: 114 us
  blocking collectives  51.3 us (45%)
  starting transfers between devices  36.6 us (32%)
  waiting for transfers between devices  16 us (14%)
  local copies, waits for them, and re-layouts  3.96 us (3%)
  Pallas kernels  3.77 us (3%)
    all_to_all x3, blocking collectives, exchange(): return lax.all_to_all(x, axes, split_axis=0, concat_axis=0, tiled=True)  51.3 us
    all_to_all x1, starting transfers between devices, exchange(): return lax.all_to_all(x, axes, split_axis=0, concat_axis=0, tiled=True)  15.7 us
    ppermute x1, waiting for transfers between devices, local(): told_after = lax.ppermute(to_last, CHAIN, down)  6.65 us
    ppermute x1, starting transfers between devices, local(): told_before = lax.ppermute(to_next, CHAIN, up)  6.65 us
    ppermute x1, waiting for transfers between devices, rims(): after = lax.ppermute(field[:, :RIM], CHAIN, down)  6.29 us
    ppermute x1, starting transfers between devices, rims(): before = lax.ppermute(field[:, width - RIM:], CHAIN, up)  4.58 us
    ppermute x1, starting transfers between devices, local(): before = lax.ppermute(upper, CHAIN, up)  3.93 us
    pallas_call x6, Pallas kernels, call(): pl.pallas_call(kernel, out_shape=shapes, in_specs=[pl.BlockSpec(memory_sp...  3.77 us
  transfers between devices with their start and end apart: 7, of which 3 were waited for; matrix products, arithmetic and copies ran while one was open for 1% of the time, Pallas kernels for 0%

profile of v3, /device:TPU:24, one launch (start us, length us, event | category | flops | bytes accessed | tf_op | source)
XLA Modules:
  0.0 113.5 jit_solution(17150860450747924790)
XLA Ops:
  0.6 0.0 copy-start
  0.6 0.9 fusion.15
  1.5 3.9 %collective-permute-start = (f32[8,256]{1,0:T(8,128)S(1)}, f32[8,256]{1,0:T(8,128)S(1)}, u32[]{:S(2)}, u32[]{:S(2)}) collective-permute-start(f32[8,256]{1,0:T(8,128)S(1)} %get-tuple-element.40.upper), channel_id=1, source_target_pairs={{0,1},{1,2},{2,3},{3,4},{4,5},{5,6},{6,7},{7,8},{8,9},{9,10},{10,1... | collective-permute-start | bytes 24584 | tf_op jit(solution)/shard_map/ppermute | solution.py:176
  5.4 1.9 %collective-permute-start.1 = (f32[8,256]{1,0:T(8,128)S(1)}, f32[8,256]{1,0:T(8,128)S(1)}, u32[]{:S(2)}, u32[]{:S(2)}) collective-permute-start(f32[8,256]{1,0:T(8,128)S(1)} %get-tuple-element.41.lower), channel_id=1, source_target_pairs={{1,0},{2,1},{3,2},{4,3},{5,4},{6,5},{7,6},{8,7},{9,8},{10,9},{11,1... | collective-permute-start | bytes 24584 | tf_op jit(solution)/shard_map/ppermute | solution.py:177
  7.4 0.7 slice.35.middle
  8.1 0.0 copy-start.1
  8.1 0.9 copy-done.1
  9.0 0.0 copy-start.2
  9.0 0.8 copy-done.2
  9.8 0.0 copy-start.3
  9.8 0.7 copy-done.3
  10.5 0.1 shard_map.77
  10.6 0.0 collective-permute-done.before
  10.6 3.1 %collective-permute-done.1.after = f32[8,256]{1,0:T(8,128)S(1)} collective-permute-done((f32[8,256]{1,0:T(8,128)S(1)}, f32[8,256]{1,0:T(8,128)S(1)}, u32[]{:S(2)}, u32[]{:S(2)}) %collective-permute-start.1) | collective-permute-done | bytes 8224 | tf_op jit(solution)/shard_map/ppermute | solution.py:177
  13.7 0.5 shard_map.78
  14.2 17.8 %all_to_all.20.arrived = f32[32,8,128]{2,1,0:T(8,128)S(1)} all-to-all(f32[32,8,128]{2,1,0:T(8,128)S(1)} %get-tuple-element.21), channel_id=1, replica_groups=mesh['yh'=2,'x'=4,'c'=2,'z'=12,'yl'=4] {'yh','x','yl'}, dimensions={0} | all-to-all | bytes 262144 | tf_op jit(solution)/shard_map/all_to_all | solution.py:28
  32.0 0.7 shard_map.79
  32.7 15.7 %all-to-all-start.1 = ((f32[24,3,4,128]{3,2,1,0:T(4,128)}), f32[24,3,4,128]{3,2,1,0:T(4,128)S(1)}, u32[]{:S(2)}, u32[]{:S(2)}) async-start(f32[24,3,4,128]{3,2,1,0:T(4,128)} %shard_map.79), calls=%async_computation.1 | async-start | bytes 294912 | tf_op jit(solution)/shard_map/all_to_all | solution.py:28
  48.4 0.0 copy-done
  48.4 0.4 fusion.8.neumann_part
  48.8 6.6 %collective-permute-start.2 = (f32[40,256]{1,0:T(8,128)S(1)}, f32[40,256]{1,0:T(8,128)S(1)}, u32[]{:S(2)}, u32[]{:S(2)}) collective-permute-start(f32[40,256]{1,0:T(8,128)S(1)} %pad_maximum_fusion), channel_id=1, source_target_pairs={{0,1},{1,2},{2,3},{3,4},{4,5},{5,6},{6,7},{7,8},{8,9},{9,10},{10,1... | collective-permute-start | bytes 122888 | tf_op jit(solution)/shard_map/ppermute | solution.py:199
  55.5 1.9 %collective-permute-start.3 = (f32[40,256]{1,0:T(8,128)S(1)}, f32[40,256]{1,0:T(8,128)S(1)}, u32[]{:S(2)}, u32[]{:S(2)}) collective-permute-start(f32[40,256]{1,0:T(8,128)S(1)} %pad_maximum_fusion.1), channel_id=1, source_target_pairs={{1,0},{2,1},{3,2},{4,3},{5,4},{6,5},{7,6},{8,7},{9,8},{10,9},{11,1... | collective-permute-start | bytes 122888 | tf_op jit(solution)/shard_map/ppermute | solution.py:200
  57.4 0.0 collective-permute-done.2.before
  57.4 6.7 %collective-permute-done.3.after = f32[40,256]{1,0:T(8,128)S(1)} collective-permute-done((f32[40,256]{1,0:T(8,128)S(1)}, f32[40,256]{1,0:T(8,128)S(1)}, u32[]{:S(2)}, u32[]{:S(2)}) %collective-permute-start.3) | collective-permute-done | bytes 40992 | tf_op jit(solution)/shard_map/ppermute | solution.py:200
  64.1 0.0 all-to-all-done.1.arrived
  64.1 0.2 shard_map.80
  64.3 12.9 %all_to_all.21.arrived = f32[32,8,128]{2,1,0:T(8,128)S(1)} all-to-all(f32[32,8,128]{2,1,0:T(8,128)S(1)} %shard_map.80), channel_id=1, replica_groups=mesh['yh'=2,'x'=4,'c'=2,'z'=12,'yl'=4] {'yh','x','yl'}, dimensions={0} | all-to-all | bytes 262144 | tf_op jit(solution)/shard_map/all_to_all | solution.py:28
  77.3 20.6 %all_to_all.22.value = f32[24,8,128]{2,1,0:T(8,128)S(1)} all-to-all(f32[24,8,128]{2,1,0:T(8,128)S(1)} %shard_map.81), channel_id=1, replica_groups=mesh['yh'=2,'x'=4,'c'=2,'z'=12,'yl'=4] {'z','c'}, dimensions={0} | all-to-all | bytes 196608 | tf_op jit(solution)/shard_map/all_to_all | solution.py:28
  97.9 2.2 %shard_map.82 = (f32[8,1024]{1,0:T(8,128)}, f32[8,1024]{1,0:T(8,128)S(1)}) custom-call(f32[24,8,128]{2,1,0:T(8,128)S(1)} %all_to_all.22.value, f32[1,128]{1,0:T(1,128)S(1)} %get-tuple-element.29.names, f32[24,1024]{1,0:T(8,128)S(1)} %get-tuple-element.18.scaled_basis, f32[8,1024]{1,0:T(8,128)S(1)} %fusion.8.neumann_part, ...), custom_call_target="tpu_custom_call" | custom-call | tf_op jit(solution)/shard_map/pallas_call | solution.py:143
  100.0 4.6 %collective-permute-start.4 = (f32[8,256]{1,0:T(8,128)S(1)}, f32[8,256]{1,0:T(8,128)S(1)}, u32[]{:S(2)}, u32[]{:S(2)}) collective-permute-start(f32[8,256]{1,0:T(8,128)S(1)} %get-tuple-element.36), channel_id=1, source_target_pairs={{0,1},{1,2},{2,3},{3,4},{4,5},{5,6},{6,7},{7,8},{8,9},{9,10},{10,1... | collective-permute-start | bytes 24584 | tf_op jit(solution)/shard_map/ppermute | solution.py:166
  104.6 1.9 %collective-permute-start.5 = (f32[8,256]{1,0:T(8,128)S(1)}, f32[8,256]{1,0:T(8,128)S(1)}, u32[]{:S(2)}, u32[]{:S(2)}) collective-permute-start(f32[8,256]{1,0:T(8,128)S(1)} %get-tuple-element.37), channel_id=1, source_target_pairs={{1,0},{2,1},{3,2},{4,3},{5,4},{6,5},{7,6},{8,7},{9,8},{10,9},{11,1... | collective-permute-start | bytes 24584 | tf_op jit(solution)/shard_map/ppermute | solution.py:167
  106.6 0.0 collective-permute-done.4
  106.6 6.3 %collective-permute-done.5 = f32[8,256]{1,0:T(8,128)S(1)} collective-permute-done((f32[8,256]{1,0:T(8,128)S(1)}, f32[8,256]{1,0:T(8,128)S(1)}, u32[]{:S(2)}, u32[]{:S(2)}) %collective-permute-start.5) | collective-permute-done | bytes 8224 | tf_op jit(solution)/shard_map/ppermute | solution.py:167
  112.9 0.6 fusion.11
  (8 shorter events, 0.1 us)
Async XLA Ops:
  0.6 47.8 %copy-start = (bf16[1,1024,1024]{2,1,0:T(8,128)(2,1)S(1)}, bf16[1,1024,1024]{2,1,0:T(8,128)(2,1)}, u32[]{:S(2)}) copy-start(bf16[1,1024,1024]{2,1,0:T(8,128)(2,1)} %param.8) | copy-start | bytes 6291460
  1.5 9.1 %collective-permute-start = (f32[8,256]{1,0:T(8,128)S(1)}, f32[8,256]{1,0:T(8,128)S(1)}, u32[]{:S(2)}, u32[]{:S(2)}) collective-permute-start(f32[8,256]{1,0:T(8,128)S(1)} %get-tuple-element.40.upper), channel_id=1, source_target_pairs={{0,1},{1,2},{2,3},{3,4},{4,5},{5,6},{6,7},{7,8},{8,9},{9,10},{10,1... | collective-permute-start | bytes 24584 | tf_op jit(solution)/shard_map/ppermute | solution.py:176
  5.4 8.3 %collective-permute-start.1 = (f32[8,256]{1,0:T(8,128)S(1)}, f32[8,256]{1,0:T(8,128)S(1)}, u32[]{:S(2)}, u32[]{:S(2)}) collective-permute-start(f32[8,256]{1,0:T(8,128)S(1)} %get-tuple-element.41.lower), channel_id=1, source_target_pairs={{1,0},{2,1},{3,2},{4,3},{5,4},{6,5},{7,6},{8,7},{9,8},{10,9},{11,1... | collective-permute-start | bytes 24584 | tf_op jit(solution)/shard_map/ppermute | solution.py:177
  8.1 0.9 copy-start.1
  9.0 0.8 copy-start.2
  9.8 0.7 copy-start.3
  32.7 31.4 %all-to-all-start.1 = ((f32[24,3,4,128]{3,2,1,0:T(4,128)}), f32[24,3,4,128]{3,2,1,0:T(4,128)S(1)}, u32[]{:S(2)}, u32[]{:S(2)}) async-start(f32[24,3,4,128]{3,2,1,0:T(4,128)} %shard_map.79), calls=%async_computation.1 | async-start | bytes 294912 | tf_op jit(solution)/shard_map/all_to_all | solution.py:28
  48.8 8.6 %collective-permute-start.2 = (f32[40,256]{1,0:T(8,128)S(1)}, f32[40,256]{1,0:T(8,128)S(1)}, u32[]{:S(2)}, u32[]{:S(2)}) collective-permute-start(f32[40,256]{1,0:T(8,128)S(1)} %pad_maximum_fusion), channel_id=1, source_target_pairs={{0,1},{1,2},{2,3},{3,4},{4,5},{5,6},{6,7},{7,8},{8,9},{9,10},{10,1... | collective-permute-start | bytes 122888 | tf_op jit(solution)/shard_map/ppermute | solution.py:199
  55.5 8.6 %collective-permute-start.3 = (f32[40,256]{1,0:T(8,128)S(1)}, f32[40,256]{1,0:T(8,128)S(1)}, u32[]{:S(2)}, u32[]{:S(2)}) collective-permute-start(f32[40,256]{1,0:T(8,128)S(1)} %pad_maximum_fusion.1), channel_id=1, source_target_pairs={{1,0},{2,1},{3,2},{4,3},{5,4},{6,5},{7,6},{8,7},{9,8},{10,9},{11,1... | collective-permute-start | bytes 122888 | tf_op jit(solution)/shard_map/ppermute | solution.py:200
  100.0 6.5 %collective-permute-start.4 = (f32[8,256]{1,0:T(8,128)S(1)}, f32[8,256]{1,0:T(8,128)S(1)}, u32[]{:S(2)}, u32[]{:S(2)}) collective-permute-start(f32[8,256]{1,0:T(8,128)S(1)} %get-tuple-element.36), channel_id=1, source_target_pairs={{0,1},{1,2},{2,3},{3,4},{4,5},{5,6},{6,7},{7,8},{8,9},{9,10},{10,1... | collective-permute-start | bytes 24584 | tf_op jit(solution)/shard_map/ppermute | solution.py:166
  104.6 8.2 %collective-permute-start.5 = (f32[8,256]{1,0:T(8,128)S(1)}, f32[8,256]{1,0:T(8,128)S(1)}, u32[]{:S(2)}, u32[]{:S(2)}) collective-permute-start(f32[8,256]{1,0:T(8,128)S(1)} %get-tuple-element.37), channel_id=1, source_target_pairs={{1,0},{2,1},{3,2},{4,3},{5,4},{6,5},{7,6},{8,7},{9,8},{10,9},{11,1... | collective-permute-start | bytes 24584 | tf_op jit(solution)/shard_map/ppermute | solution.py:167

commit v4 on v3

v4 whole, which is shorter than its diff:
```python
import jax
import jax.numpy as jnp
from jax import lax
from jax.experimental import pallas as pl
from jax.experimental.pallas import tpu as pltpu
from jax.sharding import Mesh, PartitionSpec as P


RIM = 256
ALL = ("yh", "x", "c", "z", "yl")
SIZES = (2, 4, 2, 12, 4)
CHAIN = ("z", "yl")
ROWS = ("yh", "x", "yl")
COLS = ("z", "c")
CHAIN_LENGTH = 48
N_ROWS = 32
N_COLS = 24
SLOT_BEFORE = 32
SLOT_AFTER = 64
LANES = 128
HIGH = lax.Precision.HIGHEST
F32 = jnp.float32
BF16 = jnp.bfloat16


def exchange(x, axes):
    return lax.all_to_all(x, axes, split_axis=0, concat_axis=0, tiled=True)


def in_place(x):
    return pltpu.with_memory_space_constraint(x, pltpu.HBM)


def position_of(index):
    owner = index // 4
    group, member = owner // 48, owner % 48
    row_part = (group // 2) * 4 + member % 4
    col_part = (member // 4) * 2 + group % 2
    return row_part * LANES + col_part * 4 + index % 4


def three_parts(x):
    first = x.astype(BF16)
    rest = x - first.astype(F32)
    second = rest.astype(BF16)
    third = (rest - second.astype(F32)).astype(BF16)
    return jnp.concatenate([first.astype(F32), second.astype(F32), third.astype(F32)], axis=0).astype(BF16)


def added(x):
    return x[0:8] + x[8:16] + x[16:24]


def prepare_kernel(
    basis_from, index_from, inverse_from, loads_from, weights, scaled, place, names, up_basis, down_basis, blocks, loads,
    basis, index, inverse, sems,
):
    pairs = ((basis_from, basis), (index_from, index), (loads_from, loads), (inverse_from, inverse))
    copies = [pltpu.make_async_copy(source, target, sems.at[k]) for k, (source, target) in enumerate(pairs)]
    for copy in copies:
        copy.start()
    for copy in copies:
        copy.wait()
    width, corners = basis.shape[1], basis.shape[0]
    shared = weights[...] * basis[...]
    scaled[...] = shared
    square = (corners, corners)
    same = lax.broadcasted_iota(jnp.int32, square, 0) == lax.broadcasted_iota(jnp.int32, square, 1)
    column = jnp.sum(jnp.where(same, index[...].astype(F32), 0.0), axis=1, keepdims=True).astype(jnp.int32)
    place[...] = position_of(column)
    named = index[...].astype(F32) + 1.0
    gap = jnp.zeros((1, SLOT_BEFORE - corners), F32)
    row = jnp.concatenate([named, gap, named, gap, named, gap, jnp.zeros((1, SLOT_BEFORE), F32)], axis=1)
    lanes = lax.broadcasted_iota(jnp.int32, (1, LANES), 1)
    names[...] = jnp.where(lanes < corners, row, 0.0)
    first = lax.broadcasted_iota(jnp.int32, (8, LANES), 0) == 0
    for slot, out, rim in ((SLOT_BEFORE, up_basis, shared[:, width - RIM :]), (SLOT_AFTER, down_basis, shared[:, :RIM])):
        out[:corners] = rim
        mine = first & (lanes >= slot) & (lanes < slot + corners)
        told = jnp.where(mine, jnp.broadcast_to(row, (8, LANES)), 0.0)
        out[corners:] = jnp.concatenate([told, jnp.zeros((8, RIM - LANES), F32)], axis=1)
    for q in range(N_COLS):
        blocks[q] = inverse[:, q * LANES : (q + 1) * LANES]


def sides(odd, far, near):
    flag = odd[...] > 0.5
    return jnp.where(flag, near[...], far[...]), jnp.where(flag, far[...], near[...])


def scatter_kernel(loads, far, near, odd, weights, scaled_basis, place, force, weighted, out):
    width = loads.shape[1]
    before, after = sides(odd, far, near)
    whole = jnp.concatenate(
        [loads[:, :RIM] + before, loads[:, RIM : width - RIM], loads[:, width - RIM :] + after], axis=1
    )
    force[...] = whole
    weighted[...] = weights[...] * whole
    terms = lax.dot_general(whole, scaled_basis[...], (((1,), (1,)), ((), ())), precision=HIGH, preferred_element_type=F32)
    columns = lax.broadcasted_iota(jnp.int32, (place.shape[0], N_ROWS * LANES), 1)
    hot = (columns == place[...]).astype(F32).astype(BF16)
    dense = added(jnp.dot(three_parts(terms), hot, preferred_element_type=F32))
    for p in range(N_ROWS):
        out[p] = dense[:, p * LANES : (p + 1) * LANES]


def streamed_dot(x, matrix, held, sems, meanwhile):
    steps = matrix.shape[0] // RIM
    copies = [
        pltpu.make_async_copy(matrix.at[pl.ds(k * RIM, RIM)], held.at[pl.ds(k * RIM, RIM)], sems.at[k])
        for k in range(steps)
    ]
    for copy in copies:
        copy.start()
    x = meanwhile() if meanwhile else x
    rounded = x.astype(BF16)
    total = None
    for k, copy in enumerate(copies):
        copy.wait()
        part = jnp.dot(rounded[:, k * RIM : (k + 1) * RIM], held[k * RIM : (k + 1) * RIM], preferred_element_type=F32)
        total = part if total is None else total + part
    return x, total


def neumann_kernel(weighted, weights, odd, up_basis, down_basis, neumann, out, to_far, to_near, held, sems):
    width, cases = weighted.shape[1], weighted.shape[0]
    scaled, product = streamed_dot(weighted[...], neumann, held, sems, None)
    result = weights[...] * (0.25 * scaled + 0.0625 * product)
    out[...] = result
    flag = odd[...] > 0.5
    upper, lower = result[:, width - RIM :], result[:, :RIM]
    to_far[:cases] = jnp.where(flag, upper, lower)
    to_near[:cases] = jnp.where(flag, lower, upper)
    to_far[cases:] = jnp.where(flag, up_basis[...], down_basis[...])
    to_near[cases:] = jnp.where(flag, down_basis[...], up_basis[...])


def spread_kernel(arrived, out):
    total = jnp.sum(arrived[...], axis=0)
    out[...] = jnp.broadcast_to(total[None], out.shape)


def spread_with_blocks_kernel(arrived, blocks, out):
    total = jnp.sum(arrived[...], axis=0)
    for q in range(N_COLS):
        out[q, 0] = total[0:4]
        out[q, 1] = total[4:8]
        out[q, 2] = blocks[q]


def block_kernel(arrived, out, block):
    total = jnp.concatenate([jnp.sum(arrived[:, 0], axis=0), jnp.sum(arrived[:, 1], axis=0)], axis=0)
    for q in range(N_COLS):
        block[4 * q : 4 * q + 4] = arrived[q, 2]
    value = jnp.dot(total[:, : block.shape[0]], block[...], precision=HIGH, preferred_element_type=F32)
    out[...] = jnp.broadcast_to(value[None], out.shape)


def finish_kernel(
    value, names, scaled_basis, neumann_part, odd, far, near, schur, solution, applied, to_far, to_near, held, sems
):
    width = neumann_part.shape[1]
    cases, corners = neumann_part.shape[0], scaled_basis.shape[0]
    last = cases + corners

    def assembled():
        before, after = sides(odd, far, near)
        wanted = names[...] + before[last : last + 1, :LANES] + after[last : last + 1, :LANES]
        found = jnp.zeros((3 * cases, LANES), F32)
        for q in range(N_COLS):
            rows = lax.broadcasted_iota(jnp.int32, (LANES, LANES), 0) + (q * LANES + 1)
            hot = (rows.astype(F32) == wanted).astype(F32).astype(BF16)
            found += jnp.dot(three_parts(value[q]), hot, preferred_element_type=F32)
        picked = added(found)

        def coarse(slot, basis):
            return jnp.dot(picked[:, slot : slot + corners], basis, precision=HIGH, preferred_element_type=F32)

        u = neumann_part[...] + coarse(0, scaled_basis[...])
        lower = u[:, :RIM] + before[:cases] + coarse(SLOT_BEFORE, before[cases:last])
        upper = u[:, width - RIM :] + after[:cases] + coarse(SLOT_AFTER, after[cases:last])
        u = jnp.concatenate([lower, u[:, RIM : width - RIM], upper], axis=1)
        solution[...] = u
        return u

    u, product = streamed_dot(None, schur, held, sems, assembled)
    total = 4.0 * u + product
    applied[...] = total
    flag = odd[...] > 0.5
    upper, lower = total[:, width - RIM :], total[:, :RIM]
    to_far[...] = jnp.where(flag, upper, lower)
    to_near[...] = jnp.where(flag, lower, upper)


def call(kernel, shapes, *args, in_hbm=(), scratch=()):
    shapes = [s if isinstance(s, jax.ShapeDtypeStruct) else jax.ShapeDtypeStruct(s, F32) for s in shapes]
    return pl.pallas_call(
        kernel,
        out_shape=shapes,
        in_specs=[pl.BlockSpec(memory_space=pltpu.HBM if i in in_hbm else pltpu.VMEM) for i in range(len(args))],
        out_specs=[pl.BlockSpec(memory_space=pltpu.VMEM)] * len(shapes),
        scratch_shapes=list(scratch),
        compiler_params=pltpu.CompilerParams(vmem_limit_bytes=24 << 20),
    )(*args)


def local(loads, schur, neumann, basis, coarse_index, coarse_inverse):
    loads, schur, neumann, basis, index = loads[0], schur[0], neumann[0], basis[0], coarse_index[0]
    cases, width = loads.shape
    corners = basis.shape[0]
    position = lax.axis_index(CHAIN)
    columns = lax.broadcasted_iota(jnp.int32, (1, width), 1)
    lower_rim = (columns < RIM) & (position > 0)
    upper_rim = (columns >= width - RIM) & (position < CHAIN_LENGTH - 1)
    weights = jnp.where(lower_rim | upper_rim, 0.5, 1.0).astype(F32)
    is_odd = position % 2 == 1
    odd = jnp.broadcast_to(jnp.where(is_odd, 1.0, 0.0).astype(F32), (1, RIM))

    def swap(x, first):
        pairs = [(i, i + 1) for i in range(first, CHAIN_LENGTH - 1, 2)]
        return lax.ppermute(x, CHAIN, pairs + [(j, i) for i, j in pairs])

    lower, upper = loads[:, :RIM], loads[:, width - RIM :]
    far = swap(jnp.where(is_odd, upper, lower), 1)
    near = swap(jnp.where(is_odd, lower, upper), 0)
    own = corners + 8
    streamed = dict(scratch=(pltpu.VMEM(schur.shape, BF16), pltpu.SemaphoreType.DMA((width // RIM,))))
    scaled_basis, place, own_names, up_basis, down_basis, blocks, near_loads = call(
        prepare_kernel,
        [
            (corners, width), jax.ShapeDtypeStruct((corners, 1), jnp.int32), (1, LANES),
            (own, RIM), (own, RIM), (N_COLS, 4, LANES), (cases, width),
        ],
        *(in_place(x) for x in (basis, index[None], coarse_inverse, loads)), weights,
        in_hbm=(0, 1, 2, 3),
        scratch=(
            pltpu.VMEM((corners, width), F32), pltpu.VMEM((1, corners), jnp.int32), pltpu.VMEM(coarse_inverse.shape, F32),
            pltpu.SemaphoreType.DMA((4,)),
        ),
    )
    force, weighted, partial = call(
        scatter_kernel, [(cases, width), (cases, width), (N_ROWS, cases, LANES)],
        near_loads, far, near, odd, weights, scaled_basis, place,
    )
    arrived = exchange(partial, ROWS)
    (sent,) = call(spread_with_blocks_kernel, [(N_COLS, 3, 4, LANES)], arrived, blocks)
    weighted, sent = lax.optimization_barrier((weighted, sent))

    neumann_part, to_far, to_near = call(
        neumann_kernel, [(cases, width), (cases + own, RIM), (cases + own, RIM)],
        weighted, weights, odd, up_basis, down_basis, in_place(neumann), in_hbm=(5,), **streamed,
    )
    told_far = swap(to_far, 1)
    told_near = swap(to_near, 0)

    arrived = exchange(sent, COLS)
    (sent,) = call(
        block_kernel, [(N_ROWS, cases, LANES)], arrived, scratch=(pltpu.VMEM((4 * N_COLS, LANES), F32),)
    )
    arrived = exchange(sent, ROWS)
    (sent,) = call(spread_kernel, [(N_COLS, cases, LANES)], arrived)
    value = exchange(sent, COLS)
    u, applied, to_far, to_near = call(
        finish_kernel, [(cases, width), (cases, width), (cases, RIM), (cases, RIM)],
        value, own_names, scaled_basis, neumann_part, odd, told_far, told_near, in_place(schur), in_hbm=(7,), **streamed,
    )
    far = swap(to_far, 1)
    near = swap(to_near, 0)
    before, after = jnp.where(is_odd, near, far), jnp.where(is_odd, far, near)
    whole = jnp.concatenate(
        [applied[:, :RIM] + before, applied[:, RIM : width - RIM], applied[:, width - RIM :] + after], axis=1
    )
    return (u[None], (force - whole)[None])


def solution(mesh):
    whole = Mesh(mesh.devices.reshape(SIZES), ALL)
    specs = tuple(P(ALL, *([None] * n)) for n in (2, 2, 2, 2, 1, 1))
    outs = (P(ALL, None, None), P(ALL, None, None))
    return jax.shard_map(local, mesh=whole, in_specs=specs, out_specs=outs, check_vma=False)
```

time: 114 us -> 105 us (0.921)
  starting transfers between devices: 36.6 us -> 24.1 us
  blocking collectives: 51.3 us -> 60.1 us
  waiting for transfers between devices: 16 us -> 11.5 us
  local copies, waits for them, and re-layouts: 3.96 us -> 0.01 us
  Pallas kernels: 3.77 us -> 6.59 us
    all_to_all x1, starting transfers between devices: 15.7 us -> 3.81 us  [exchange(): return lax.all_to_all(x, axes, split_axis=0, concat_axis=0, tiled=True)]
    all_to_all x3, blocking collectives: 51.3 us -> 60.1 us  [exchange(): return lax.all_to_all(x, axes, split_axis=0, concat_axis=0, tiled=True)]
    ppermute x6, waiting for transfers between devices: 16 us -> 11.5 us  [swap(): return lax.ppermute(x, CHAIN, pairs + [(j, i) for i, j in pairs])]
    pallas_call x6 -> x7, Pallas kernels: 3.77 us -> 6.59 us  [call(): pl.pallas_call(kernel, out_shape=shapes, in_specs=[pl.BlockSpec(memory_sp...]
    unnamed x8 -> x0, local copies, waits for them, and re-layouts: 2.35 us -> none
    slice x5 -> x1, local copies, waits for them, and re-layouts: 1.6 us -> 0.01 us  [local(): applied[:, RIM:width - RIM]]
  transfers between devices with their start and end apart: 7 -> 7, of which waited for: 3 -> 5; matrix products, arithmetic and copies ran while one was open for 1% -> 0% of each run, Pallas kernels for 0% -> 3%
where the time goes in v4:
time: 105 us; the launch traced here: 104 us
  blocking collectives  60.1 us (57%)
  starting transfers between devices  24.1 us (23%)
  waiting for transfers between devices  11.5 us (11%)
  Pallas kernels  6.59 us (6%)
  other arithmetic  1.36 us (1%)
    all_to_all x3, blocking collectives, exchange(): return lax.all_to_all(x, axes, split_axis=0, concat_axis=0, tiled=True)  60.1 us
    ppermute x6, starting transfers between devices, swap(): return lax.ppermute(x, CHAIN, pairs + [(j, i) for i, j in pairs])  20.3 us
    ppermute x6, waiting for transfers between devices, swap(): return lax.ppermute(x, CHAIN, pairs + [(j, i) for i, j in pairs])  11.5 us
    pallas_call x7, Pallas kernels, call(): pl.pallas_call(kernel, out_shape=shapes, in_specs=[pl.BlockSpec(memory_sp...  6.59 us
    all_to_all x1, starting transfers between devices, exchange(): return lax.all_to_all(x, axes, split_axis=0, concat_axis=0, tiled=True)  3.81 us
  transfers between devices with their start and end apart: 7, of which 5 were waited for; matrix products, arithmetic and copies ran while one was open for 0% of the time, Pallas kernels for 3%

profile of v4, /device:TPU:24, one launch (start us, length us, event | category | flops | bytes accessed | tf_op | source)
XLA Modules:
  0.0 104.5 jit_solution(8861580333334736493)
XLA Ops:
  0.7 0.7 slice_select_fusion
  1.4 2.3 %collective-permute-start.1 = (f32[8,256]{1,0:T(8,128)S(1)}, f32[8,256]{1,0:T(8,128)S(1)}, u32[]{:S(2)}, u32[]{:S(2)}) collective-permute-start(f32[8,256]{1,0:T(8,128)S(1)} %get-tuple-element.42), channel_id=1, source_target_pairs={{0,1},{2,3},{4,5},{6,7},{8,9},{10,11},{12,13},{14,15},{16,17},{18,... | collective-permute-start | bytes 24584 | tf_op jit(solution)/shard_map/ppermute | solution.py:221
  3.7 5.1 %collective-permute-start = (f32[8,256]{1,0:T(8,128)S(1)}, f32[8,256]{1,0:T(8,128)S(1)}, u32[]{:S(2)}, u32[]{:S(2)}) collective-permute-start(f32[8,256]{1,0:T(8,128)S(1)} %get-tuple-element.43), channel_id=1, source_target_pairs={{1,2},{3,4},{5,6},{7,8},{9,10},{11,12},{13,14},{15,16},{17,18},{19... | collective-permute-start | bytes 24584 | tf_op jit(solution)/shard_map/ppermute | solution.py:221
  8.8 1.1 %shard_map.77 = (f32[24,1024]{1,0:T(8,128)S(1)}, s32[24,1]{1,0:T(8,128)S(1)}, f32[1,128]{1,0:T(1,128)S(1)}, f32[32,256]{1,0:T(8,128)S(1)}, f32[32,256]{1,0:T(8,1...) custom-call(f32[24,1024]{1,0:T(8,128)} %bitcast.9, s32[1,24]{1,0:T(1,128)} %index_from.1, ...), custom_call_target="tpu_custom_call" | custom-call | tf_op jit(solution)/shard_map/pallas_call | solution.py:197
  9.9 0.0 collective-permute-done.1.near
  9.9 2.0 %collective-permute-done.far = f32[8,256]{1,0:T(8,128)S(1)} collective-permute-done((f32[8,256]{1,0:T(8,128)S(1)}, f32[8,256]{1,0:T(8,128)S(1)}, u32[]{:S(2)}, u32[]{:S(2)}) %collective-permute-start) | collective-permute-done | bytes 8224 | tf_op jit(solution)/shard_map/ppermute | solution.py:221
  12.0 0.5 shard_map.78
  12.5 17.0 %all_to_all.20.arrived = f32[32,8,128]{2,1,0:T(8,128)S(1)} all-to-all(f32[32,8,128]{2,1,0:T(8,128)S(1)} %get-tuple-element.25), channel_id=1, replica_groups=mesh['yh'=2,'x'=4,'c'=2,'z'=12,'yl'=4] {'yh','x','yl'}, dimensions={0} | all-to-all | bytes 262144 | tf_op jit(solution)/shard_map/all_to_all | solution.py:27
  29.6 28.9 %all_to_all.21.arrived = f32[24,3,4,128]{3,2,1,0:T(4,128)S(1)} all-to-all(f32[24,3,4,128]{3,2,1,0:T(4,128)S(1)} %shard_map.79), channel_id=1, replica_groups=mesh['yh'=2,'x'=4,'c'=2,'z'=12,'yl'=4] {'z','c'}, dimensions={0} | all-to-all | bytes 294912 | tf_op jit(solution)/shard_map/all_to_all | solution.py:27
  58.5 0.2 shard_map.80
  58.7 14.2 %all_to_all.22.arrived = f32[32,8,128]{2,1,0:T(8,128)S(1)} all-to-all(f32[32,8,128]{2,1,0:T(8,128)S(1)} %shard_map.80), channel_id=1, replica_groups=mesh['yh'=2,'x'=4,'c'=2,'z'=12,'yl'=4] {'yh','x','yl'}, dimensions={0} | all-to-all | bytes 262144 | tf_op jit(solution)/shard_map/all_to_all | solution.py:27
  72.9 0.7 shard_map.81
  73.5 3.8 %all-to-all-start.3 = ((f32[24,8,128]{2,1,0:T(8,128)}), f32[24,8,128]{2,1,0:T(8,128)S(1)}, u32[]{:S(2)}, u32[]{:S(2)}) async-start(f32[24,8,128]{2,1,0:T(8,128)} %shard_map.81), calls=%async_computation.3 | async-start | bytes 196608 | tf_op jit(solution)/shard_map/all_to_all | solution.py:27
  77.4 1.7 %shard_map.82 = (f32[8,1024]{1,0:T(8,128)S(1)}, f32[40,256]{1,0:T(8,128)S(1)}, f32[40,256]{1,0:T(8,128)S(1)}) custom-call(f32[8,1024]{1,0:T(8,128)S(1)} %get-tuple-element.29.weighted, f32[1,1024]{1,0:T(1,128)S(1)} %or_select_fusion.weights, f32[1,256]{1,0:T(1,128)S(1)} %broadcast_in_dim.19.odd, f32[32,256]{1,0:T(8,128)S(1)} %get-tuple-element.30.up_basis, ...), custom_call_target="tpu_custom_call" | custom-call | tf_op jit(solution)/shard_map/pallas_call | solution.py:197
  79.1 6.3 %collective-permute-start.2 = (f32[40,256]{1,0:T(8,128)S(1)}, f32[40,256]{1,0:T(8,128)S(1)}, u32[]{:S(2)}, u32[]{:S(2)}) collective-permute-start(f32[40,256]{1,0:T(8,128)S(1)} %get-tuple-element.33), channel_id=1, source_target_pairs={{1,2},{3,4},{5,6},{7,8},{9,10},{11,12},{13,14},{15,16},{17,18},{19... | collective-permute-start | bytes 122888 | tf_op jit(solution)/shard_map/ppermute | solution.py:221
  85.4 1.9 %collective-permute-start.3 = (f32[40,256]{1,0:T(8,128)S(1)}, f32[40,256]{1,0:T(8,128)S(1)}, u32[]{:S(2)}, u32[]{:S(2)}) collective-permute-start(f32[40,256]{1,0:T(8,128)S(1)} %get-tuple-element.34), channel_id=1, source_target_pairs={{0,1},{2,3},{4,5},{6,7},{8,9},{10,11},{12,13},{14,15},{16,17},{18,... | collective-permute-start | bytes 122888 | tf_op jit(solution)/shard_map/ppermute | solution.py:221
  87.4 0.5 collective-permute-done.2.far
  87.9 3.5 %collective-permute-done.3.near = f32[40,256]{1,0:T(8,128)S(1)} collective-permute-done((f32[40,256]{1,0:T(8,128)S(1)}, f32[40,256]{1,0:T(8,128)S(1)}, u32[]{:S(2)}, u32[]{:S(2)}) %collective-permute-start.3) | collective-permute-done | bytes 40992 | tf_op jit(solution)/shard_map/ppermute | solution.py:221
  91.3 0.0 all-to-all-done.3.value
  91.3 2.4 %shard_map.83 = (f32[8,1024]{1,0:T(8,128)}, f32[8,1024]{1,0:T(8,128)S(1)}, f32[8,256]{1,0:T(8,128)S(1)}, f32[8,256]{1,0:T(8,128)S(1)}) custom-call(f32[24,8,128]{2,1,0:T(8,128)S(1)} %all-to-all-done.3.value, f32[1,128]{1,0:T(1,128)S(1)} %get-tuple-element.28.names, f32[24,1024]{1,0:T(8,128)S(1)} %get-tuple-element.22.scaled_basis, ...), custom_call_target="tpu_custom_call" | custom-call | tf_op jit(solution)/shard_map/pallas_call | solution.py:197
  93.7 1.9 %collective-permute-start.4 = (f32[8,256]{1,0:T(8,128)S(1)}, f32[8,256]{1,0:T(8,128)S(1)}, u32[]{:S(2)}, u32[]{:S(2)}) collective-permute-start(f32[8,256]{1,0:T(8,128)S(1)} %get-tuple-element.38), channel_id=1, source_target_pairs={{0,1},{2,3},{4,5},{6,7},{8,9},{10,11},{12,13},{14,15},{16,17},{18,... | collective-permute-start | bytes 24584 | tf_op jit(solution)/shard_map/ppermute | solution.py:221
  95.6 2.7 %collective-permute-start.5 = (f32[8,256]{1,0:T(8,128)S(1)}, f32[8,256]{1,0:T(8,128)S(1)}, u32[]{:S(2)}, u32[]{:S(2)}) collective-permute-start(f32[8,256]{1,0:T(8,128)S(1)} %get-tuple-element.39), channel_id=1, source_target_pairs={{1,2},{3,4},{5,6},{7,8},{9,10},{11,12},{13,14},{15,16},{17,18},{19... | collective-permute-start | bytes 24584 | tf_op jit(solution)/shard_map/ppermute | solution.py:221
  98.4 0.9 collective-permute-done.4
  99.2 4.6 %collective-permute-done.5 = f32[8,256]{1,0:T(8,128)S(1)} collective-permute-done((f32[8,256]{1,0:T(8,128)S(1)}, f32[8,256]{1,0:T(8,128)S(1)}, u32[]{:S(2)}, u32[]{:S(2)}) %collective-permute-start.5) | collective-permute-done | bytes 8224 | tf_op jit(solution)/shard_map/ppermute | solution.py:221
  103.9 0.6 fusion
  (5 shorter events, 0.1 us)
Async XLA Ops:
  1.4 8.5 %collective-permute-start.1 = (f32[8,256]{1,0:T(8,128)S(1)}, f32[8,256]{1,0:T(8,128)S(1)}, u32[]{:S(2)}, u32[]{:S(2)}) collective-permute-start(f32[8,256]{1,0:T(8,128)S(1)} %get-tuple-element.42), channel_id=1, source_target_pairs={{0,1},{2,3},{4,5},{6,7},{8,9},{10,11},{12,13},{14,15},{16,17},{18,... | collective-permute-start | bytes 24584 | tf_op jit(solution)/shard_map/ppermute | solution.py:221
  3.7 8.2 %collective-permute-start = (f32[8,256]{1,0:T(8,128)S(1)}, f32[8,256]{1,0:T(8,128)S(1)}, u32[]{:S(2)}, u32[]{:S(2)}) collective-permute-start(f32[8,256]{1,0:T(8,128)S(1)} %get-tuple-element.43), channel_id=1, source_target_pairs={{1,2},{3,4},{5,6},{7,8},{9,10},{11,12},{13,14},{15,16},{17,18},{19... | collective-permute-start | bytes 24584 | tf_op jit(solution)/shard_map/ppermute | solution.py:221
  73.5 17.8 %all-to-all-start.3 = ((f32[24,8,128]{2,1,0:T(8,128)}), f32[24,8,128]{2,1,0:T(8,128)S(1)}, u32[]{:S(2)}, u32[]{:S(2)}) async-start(f32[24,8,128]{2,1,0:T(8,128)} %shard_map.81), calls=%async_computation.3 | async-start | bytes 196608 | tf_op jit(solution)/shard_map/all_to_all | solution.py:27
  79.1 8.8 %collective-permute-start.2 = (f32[40,256]{1,0:T(8,128)S(1)}, f32[40,256]{1,0:T(8,128)S(1)}, u32[]{:S(2)}, u32[]{:S(2)}) collective-permute-start(f32[40,256]{1,0:T(8,128)S(1)} %get-tuple-element.33), channel_id=1, source_target_pairs={{1,2},{3,4},{5,6},{7,8},{9,10},{11,12},{13,14},{15,16},{17,18},{19... | collective-permute-start | bytes 122888 | tf_op jit(solution)/shard_map/ppermute | solution.py:221
  85.4 5.9 %collective-permute-start.3 = (f32[40,256]{1,0:T(8,128)S(1)}, f32[40,256]{1,0:T(8,128)S(1)}, u32[]{:S(2)}, u32[]{:S(2)}) collective-permute-start(f32[40,256]{1,0:T(8,128)S(1)} %get-tuple-element.34), channel_id=1, source_target_pairs={{0,1},{2,3},{4,5},{6,7},{8,9},{10,11},{12,13},{14,15},{16,17},{18,... | collective-permute-start | bytes 122888 | tf_op jit(solution)/shard_map/ppermute | solution.py:221
  93.7 5.5 %collective-permute-start.4 = (f32[8,256]{1,0:T(8,128)S(1)}, f32[8,256]{1,0:T(8,128)S(1)}, u32[]{:S(2)}, u32[]{:S(2)}) collective-permute-start(f32[8,256]{1,0:T(8,128)S(1)} %get-tuple-element.38), channel_id=1, source_target_pairs={{0,1},{2,3},{4,5},{6,7},{8,9},{10,11},{12,13},{14,15},{16,17},{18,... | collective-permute-start | bytes 24584 | tf_op jit(solution)/shard_map/ppermute | solution.py:221
  95.6 8.2 %collective-permute-start.5 = (f32[8,256]{1,0:T(8,128)S(1)}, f32[8,256]{1,0:T(8,128)S(1)}, u32[]{:S(2)}, u32[]{:S(2)}) collective-permute-start(f32[8,256]{1,0:T(8,128)S(1)} %get-tuple-element.39), channel_id=1, source_target_pairs={{1,2},{3,4},{5,6},{7,8},{9,10},{11,12},{13,14},{15,16},{17,18},{19... | collective-permute-start | bytes 24584 | tf_op jit(solution)/shard_map/ppermute | solution.py:221

commit v5 on v4

--- a/solution.py
+++ b/solution.py
@@ -104,27 +104,31 @@
         out[p] = dense[:, p * LANES : (p + 1) * LANES]
 
 
-def streamed_dot(x, matrix, held, sems, meanwhile):
-    steps = matrix.shape[0] // RIM
+def streamed_dot(x, matrix, held, sems):
     copies = [
         pltpu.make_async_copy(matrix.at[pl.ds(k * RIM, RIM)], held.at[pl.ds(k * RIM, RIM)], sems.at[k])
-        for k in range(steps)
+        for k in range(matrix.shape[0] // RIM)
     ]
     for copy in copies:
         copy.start()
-    x = meanwhile() if meanwhile else x
-    rounded = x.astype(BF16)
     total = None
     for k, copy in enumerate(copies):
         copy.wait()
-        part = jnp.dot(rounded[:, k * RIM : (k + 1) * RIM], held[k * RIM : (k + 1) * RIM], preferred_element_type=F32)
+        part = jnp.dot(x[:, k * RIM : (k + 1) * RIM], held[k * RIM : (k + 1) * RIM], preferred_element_type=F32)
         total = part if total is None else total + part
-    return x, total
+    return total
+
+
+def fetch_kernel(matrix, out, sem):
+    copy = pltpu.make_async_copy(matrix, out, sem.at[0])
+    copy.start()
+    copy.wait()
 
 
 def neumann_kernel(weighted, weights, odd, up_basis, down_basis, neumann, out, to_far, to_near, held, sems):
     width, cases = weighted.shape[1], weighted.shape[0]
-    scaled, product = streamed_dot(weighted[...], neumann, held, sems, None)
+    scaled = weighted[...]
+    product = streamed_dot(scaled.astype(BF16), neumann, held, sems)
     result = weights[...] * (0.25 * scaled + 0.0625 * product)
     out[...] = result
     flag = odd[...] > 0.5
@@ -157,7 +161,7 @@
 
 
 def finish_kernel(
-    value, names, scaled_basis, neumann_part, odd, far, near, schur, solution, applied, to_far, to_near, held, sems
+    value, names, scaled_basis, neumann_part, odd, far, near, schur, solution, applied, to_far, to_near
 ):
     width = neumann_part.shape[1]
     cases, corners = neumann_part.shape[0], scaled_basis.shape[0]
@@ -183,8 +187,8 @@
         solution[...] = u
         return u
 
-    u, product = streamed_dot(None, schur, held, sems, assembled)
-    total = 4.0 * u + product
+    u = assembled()
+    total = 4.0 * u + jnp.dot(u.astype(BF16), schur[...], preferred_element_type=F32)
     applied[...] = total
     flag = odd[...] > 0.5
     upper, lower = total[:, width - RIM :], total[:, :RIM]
@@ -253,7 +257,12 @@
     told_far = swap(to_far, 1)
     told_near = swap(to_near, 0)
 
+    (fetched,) = call(
+        fetch_kernel, [jax.ShapeDtypeStruct(schur.shape, BF16)], in_place(schur), in_hbm=(0,),
+        scratch=(pltpu.SemaphoreType.DMA((1,)),),
+    )
     arrived = exchange(sent, COLS)
+    arrived, told_far, told_near = lax.optimization_barrier((arrived, told_far, told_near))
     (sent,) = call(
         block_kernel, [(N_ROWS, cases, LANES)], arrived, scratch=(pltpu.VMEM((4 * N_COLS, LANES), F32),)
     )
@@ -262,7 +271,7 @@
     value = exchange(sent, COLS)
     u, applied, to_far, to_near = call(
         finish_kernel, [(cases, width), (cases, width), (cases, RIM), (cases, RIM)],
-        value, own_names, scaled_basis, neumann_part, odd, told_far, told_near, in_place(schur), in_hbm=(7,), **streamed,
+        value, own_names, scaled_basis, neumann_part, odd, told_far, told_near, fetched,
     )
     far = swap(to_far, 1)
     near = swap(to_near, 0)

time: 105 us -> 109 us (1.038)
  blocking collectives: 60.1 us -> 30 us
  starting transfers between devices: 24.1 us -> 48.1 us
  waiting for transfers between devices: 11.5 us -> 20.3 us
  Pallas kernels: 6.59 us -> 7.7 us
    all_to_all x3 -> x2, blocking collectives: 60.1 us -> 30 us  [exchange(): return lax.all_to_all(x, axes, split_axis=0, concat_axis=0, tiled=True)]
    all_to_all x1 -> x2, starting transfers between devices: 3.81 us -> 25 us  [exchange(): return lax.all_to_all(x, axes, split_axis=0, concat_axis=0, tiled=True)]
    all_to_all x1 -> x2, waiting for transfers between devices: 0.01 us -> 9.88 us  [exchange(): return lax.all_to_all(x, axes, split_axis=0, concat_axis=0, tiled=True)]
    ppermute x6, starting transfers between devices: 20.3 us -> 23 us  [swap(): return lax.ppermute(x, CHAIN, pairs + [(j, i) for i, j in pairs])]
    pallas_call x7 -> x8, Pallas kernels: 6.59 us -> 7.7 us  [call(): pl.pallas_call(kernel, out_shape=shapes, in_specs=[pl.BlockSpec(memory_sp...]
  transfers between devices with their start and end apart: 7 -> 8, of which waited for: 5 -> 5; matrix products, arithmetic and copies ran while one was open for 0% -> 0% of each run, Pallas kernels for 3% -> 4%
where the time goes in v5:
time: 109 us; the launch traced here: 108 us
  starting transfers between devices  48.1 us (44%)
  blocking collectives  30 us (28%)
  waiting for transfers between devices  20.3 us (19%)
  Pallas kernels  7.7 us (7%)
  other arithmetic  1.36 us (1%)
    all_to_all x2, blocking collectives, exchange(): return lax.all_to_all(x, axes, split_axis=0, concat_axis=0, tiled=True)  30 us
    all_to_all x2, starting transfers between devices, exchange(): return lax.all_to_all(x, axes, split_axis=0, concat_axis=0, tiled=True)  25 us
    ppermute x6, starting transfers between devices, swap(): return lax.ppermute(x, CHAIN, pairs + [(j, i) for i, j in pairs])  23 us
    ppermute x6, waiting for transfers between devices, swap(): return lax.ppermute(x, CHAIN, pairs + [(j, i) for i, j in pairs])  10.5 us
    all_to_all x2, waiting for transfers between devices, exchange(): return lax.all_to_all(x, axes, split_axis=0, concat_axis=0, tiled=True)  9.88 us
    pallas_call x8, Pallas kernels, call(): pl.pallas_call(kernel, out_shape=shapes, in_specs=[pl.BlockSpec(memory_sp...  7.7 us
  transfers between devices with their start and end apart: 8, of which 5 were waited for; matrix products, arithmetic and copies ran while one was open for 0% of the time, Pallas kernels for 4%

profile of v5, /device:TPU:24, one launch (start us, length us, event | category | flops | bytes accessed | tf_op | source)
XLA Modules:
  0.0 108.2 jit_solution(1695422436133815215)
XLA Ops:
  0.7 0.7 slice_select_fusion
  1.4 2.3 %collective-permute-start.1 = (f32[8,256]{1,0:T(8,128)S(1)}, f32[8,256]{1,0:T(8,128)S(1)}, u32[]{:S(2)}, u32[]{:S(2)}) collective-permute-start(f32[8,256]{1,0:T(8,128)S(1)} %get-tuple-element.48), channel_id=1, source_target_pairs={{0,1},{2,3},{4,5},{6,7},{8,9},{10,11},{12,13},{14,15},{16,17},{18,... | collective-permute-start | bytes 24584 | tf_op jit(solution)/shard_map/ppermute | solution.py:225
  3.7 5.1 %collective-permute-start = (f32[8,256]{1,0:T(8,128)S(1)}, f32[8,256]{1,0:T(8,128)S(1)}, u32[]{:S(2)}, u32[]{:S(2)}) collective-permute-start(f32[8,256]{1,0:T(8,128)S(1)} %get-tuple-element.49), channel_id=1, source_target_pairs={{1,2},{3,4},{5,6},{7,8},{9,10},{11,12},{13,14},{15,16},{17,18},{19... | collective-permute-start | bytes 24584 | tf_op jit(solution)/shard_map/ppermute | solution.py:225
  8.8 1.1 shard_map.77
  9.9 0.0 collective-permute-done.1.near
  9.9 2.0 %collective-permute-done.far = f32[8,256]{1,0:T(8,128)S(1)} collective-permute-done((f32[8,256]{1,0:T(8,128)S(1)}, f32[8,256]{1,0:T(8,128)S(1)}, u32[]{:S(2)}, u32[]{:S(2)}) %collective-permute-start) | collective-permute-done | bytes 8224 | tf_op jit(solution)/shard_map/ppermute | solution.py:225
  12.0 0.5 shard_map.78
  12.5 17.0 %all_to_all.20.arrived = f32[32,8,128]{2,1,0:T(8,128)S(1)} all-to-all(f32[32,8,128]{2,1,0:T(8,128)S(1)} %get-tuple-element.28), channel_id=1, replica_groups=mesh['yh'=2,'x'=4,'c'=2,'z'=12,'yl'=4] {'yh','x','yl'}, dimensions={0} | all-to-all | bytes 262144 | tf_op jit(solution)/shard_map/all_to_all | solution.py:27
  29.5 0.7 shard_map.79
  30.2 16.0 %all-to-all-start.1 = ((f32[24,3,4,128]{3,2,1,0:T(4,128)}), f32[24,3,4,128]{3,2,1,0:T(4,128)S(1)}, u32[]{:S(2)}, u32[]{:S(2)}) async-start(f32[24,3,4,128]{3,2,1,0:T(4,128)} %shard_map.79), calls=%async_computation.1 | async-start | bytes 294912 | tf_op jit(solution)/shard_map/all_to_all | solution.py:27
  46.3 1.7 %shard_map.80 = (f32[8,1024]{1,0:T(8,128)S(1)}, f32[40,256]{1,0:T(8,128)S(1)}, f32[40,256]{1,0:T(8,128)S(1)}) custom-call(f32[8,1024]{1,0:T(8,128)S(1)} %get-tuple-element.31.weighted, f32[1,1024]{1,0:T(1,128)S(1)} %or_select_fusion.weights, f32[1,256]{1,0:T(1,128)S(1)} %broadcast_in_dim.19.odd, f32[32,256]{1,0:T(8,128)S(1)} %get-tuple-element.32.up_basis, ...), custom_call_target="tpu_custom_call" | custom-call | tf_op jit(solution)/shard_map/pallas_call | solution.py:201
  48.0 6.6 %collective-permute-start.2 = (f32[40,256]{1,0:T(8,128)S(1)}, f32[40,256]{1,0:T(8,128)S(1)}, u32[]{:S(2)}, u32[]{:S(2)}) collective-permute-start(f32[40,256]{1,0:T(8,128)S(1)} %get-tuple-element.34), channel_id=1, source_target_pairs={{1,2},{3,4},{5,6},{7,8},{9,10},{11,12},{13,14},{15,16},{17,18},{19... | collective-permute-start | bytes 122888 | tf_op jit(solution)/shard_map/ppermute | solution.py:225
  54.7 1.9 %collective-permute-start.3 = (f32[40,256]{1,0:T(8,128)S(1)}, f32[40,256]{1,0:T(8,128)S(1)}, u32[]{:S(2)}, u32[]{:S(2)}) collective-permute-start(f32[40,256]{1,0:T(8,128)S(1)} %get-tuple-element.35), channel_id=1, source_target_pairs={{0,1},{2,3},{4,5},{6,7},{8,9},{10,11},{12,13},{14,15},{16,17},{18,... | collective-permute-start | bytes 122888 | tf_op jit(solution)/shard_map/ppermute | solution.py:225
  56.6 0.5 collective-permute-done.2.far
  57.1 3.5 %collective-permute-done.3.near = f32[40,256]{1,0:T(8,128)S(1)} collective-permute-done((f32[40,256]{1,0:T(8,128)S(1)}, f32[40,256]{1,0:T(8,128)S(1)}, u32[]{:S(2)}, u32[]{:S(2)}) %collective-permute-start.3) | collective-permute-done | bytes 40992 | tf_op jit(solution)/shard_map/ppermute | solution.py:225
  60.6 0.0 all-to-all-done.1.arrived
  60.6 0.2 shard_map.81
  60.8 12.9 %all_to_all.21.arrived = f32[32,8,128]{2,1,0:T(8,128)S(1)} all-to-all(f32[32,8,128]{2,1,0:T(8,128)S(1)} %shard_map.81), channel_id=1, replica_groups=mesh['yh'=2,'x'=4,'c'=2,'z'=12,'yl'=4] {'yh','x','yl'}, dimensions={0} | all-to-all | bytes 262144 | tf_op jit(solution)/shard_map/all_to_all | solution.py:27
  73.7 0.7 shard_map.82
  74.4 9.0 %all-to-all-start.3 = ((f32[24,8,128]{2,1,0:T(8,128)}), f32[24,8,128]{2,1,0:T(8,128)S(1)}, u32[]{:S(2)}, u32[]{:S(2)}) async-start(f32[24,8,128]{2,1,0:T(8,128)} %shard_map.82), calls=%async_computation.3 | async-start | bytes 196608 | tf_op jit(solution)/shard_map/all_to_all | solution.py:27
  83.4 1.6 %shard_map.83.schur = bf16[1024,1024]{1,0:T(8,128)(2,1)S(1)} custom-call(bf16[1024,1024]{1,0:T(8,128)(2,1)} %bitcast.8), custom_call_target="tpu_custom_call" | custom-call | tf_op jit(solution)/shard_map/pallas_call | solution.py:201
  85.0 9.9 %all-to-all-done.3.value = f32[24,8,128]{2,1,0:T(8,128)S(1)} async-done(((f32[24,8,128]{2,1,0:T(8,128)}), f32[24,8,128]{2,1,0:T(8,128)S(1)}, u32[]{:S(2)}, u32[]{:S(2)}) %all-to-all-start.3) | async-done | bytes 98336 | tf_op jit(solution)/shard_map/all_to_all | solution.py:27
  94.9 1.2 %shard_map.84 = (f32[8,1024]{1,0:T(8,128)}, f32[8,1024]{1,0:T(8,128)S(1)}, f32[8,256]{1,0:T(8,128)S(1)}, f32[8,256]{1,0:T(8,128)S(1)}) custom-call(f32[24,8,128]{2,1,0:T(8,128)S(1)} %all-to-all-done.3.value, f32[1,128]{1,0:T(1,128)S(1)} %get-tuple-element.37.names, f32[24,1024]{1,0:T(8,128)S(1)} %get-tuple-element.25.scaled_basis, ...), custom_call_target="tpu_custom_call" | custom-call | tf_op jit(solution)/shard_map/pallas_call | solution.py:201
  96.1 3.3 %collective-permute-start.4 = (f32[8,256]{1,0:T(8,128)S(1)}, f32[8,256]{1,0:T(8,128)S(1)}, u32[]{:S(2)}, u32[]{:S(2)}) collective-permute-start(f32[8,256]{1,0:T(8,128)S(1)} %get-tuple-element.44), channel_id=1, source_target_pairs={{0,1},{2,3},{4,5},{6,7},{8,9},{10,11},{12,13},{14,15},{16,17},{18,... | collective-permute-start | bytes 24584 | tf_op jit(solution)/shard_map/ppermute | solution.py:225
  99.4 3.8 %collective-permute-start.5 = (f32[8,256]{1,0:T(8,128)S(1)}, f32[8,256]{1,0:T(8,128)S(1)}, u32[]{:S(2)}, u32[]{:S(2)}) collective-permute-start(f32[8,256]{1,0:T(8,128)S(1)} %get-tuple-element.45), channel_id=1, source_target_pairs={{1,2},{3,4},{5,6},{7,8},{9,10},{11,12},{13,14},{15,16},{17,18},{19... | collective-permute-start | bytes 24584 | tf_op jit(solution)/shard_map/ppermute | solution.py:225
  103.1 0.0 collective-permute-done.4
  103.2 4.5 %collective-permute-done.5 = f32[8,256]{1,0:T(8,128)S(1)} collective-permute-done((f32[8,256]{1,0:T(8,128)S(1)}, f32[8,256]{1,0:T(8,128)S(1)}, u32[]{:S(2)}, u32[]{:S(2)}) %collective-permute-start.5) | collective-permute-done | bytes 8224 | tf_op jit(solution)/shard_map/ppermute | solution.py:225
  107.6 0.6 fusion
  (4 shorter events, 0.0 us)
Async XLA Ops:
  1.4 8.5 %collective-permute-start.1 = (f32[8,256]{1,0:T(8,128)S(1)}, f32[8,256]{1,0:T(8,128)S(1)}, u32[]{:S(2)}, u32[]{:S(2)}) collective-permute-start(f32[8,256]{1,0:T(8,128)S(1)} %get-tuple-element.48), channel_id=1, source_target_pairs={{0,1},{2,3},{4,5},{6,7},{8,9},{10,11},{12,13},{14,15},{16,17},{18,... | collective-permute-start | bytes 24584 | tf_op jit(solution)/shard_map/ppermute | solution.py:225
  3.7 8.2 %collective-permute-start = (f32[8,256]{1,0:T(8,128)S(1)}, f32[8,256]{1,0:T(8,128)S(1)}, u32[]{:S(2)}, u32[]{:S(2)}) collective-permute-start(f32[8,256]{1,0:T(8,128)S(1)} %get-tuple-element.49), channel_id=1, source_target_pairs={{1,2},{3,4},{5,6},{7,8},{9,10},{11,12},{13,14},{15,16},{17,18},{19... | collective-permute-start | bytes 24584 | tf_op jit(solution)/shard_map/ppermute | solution.py:225
  30.2 30.3 %all-to-all-start.1 = ((f32[24,3,4,128]{3,2,1,0:T(4,128)}), f32[24,3,4,128]{3,2,1,0:T(4,128)S(1)}, u32[]{:S(2)}, u32[]{:S(2)}) async-start(f32[24,3,4,128]{3,2,1,0:T(4,128)} %shard_map.79), calls=%async_computation.1 | async-start | bytes 294912 | tf_op jit(solution)/shard_map/all_to_all | solution.py:27
  48.0 9.1 %collective-permute-start.2 = (f32[40,256]{1,0:T(8,128)S(1)}, f32[40,256]{1,0:T(8,128)S(1)}, u32[]{:S(2)}, u32[]{:S(2)}) collective-permute-start(f32[40,256]{1,0:T(8,128)S(1)} %get-tuple-element.34), channel_id=1, source_target_pairs={{1,2},{3,4},{5,6},{7,8},{9,10},{11,12},{13,14},{15,16},{17,18},{19... | collective-permute-start | bytes 122888 | tf_op jit(solution)/shard_map/ppermute | solution.py:225
  54.7 5.9 %collective-permute-start.3 = (f32[40,256]{1,0:T(8,128)S(1)}, f32[40,256]{1,0:T(8,128)S(1)}, u32[]{:S(2)}, u32[]{:S(2)}) collective-permute-start(f32[40,256]{1,0:T(8,128)S(1)} %get-tuple-element.35), channel_id=1, source_target_pairs={{0,1},{2,3},{4,5},{6,7},{8,9},{10,11},{12,13},{14,15},{16,17},{18,... | collective-permute-start | bytes 122888 | tf_op jit(solution)/shard_map/ppermute | solution.py:225
  74.4 20.5 %all-to-all-start.3 = ((f32[24,8,128]{2,1,0:T(8,128)}), f32[24,8,128]{2,1,0:T(8,128)S(1)}, u32[]{:S(2)}, u32[]{:S(2)}) async-start(f32[24,8,128]{2,1,0:T(8,128)} %shard_map.82), calls=%async_computation.3 | async-start | bytes 196608 | tf_op jit(solution)/shard_map/all_to_all | solution.py:27
  96.1 7.1 %collective-permute-start.4 = (f32[8,256]{1,0:T(8,128)S(1)}, f32[8,256]{1,0:T(8,128)S(1)}, u32[]{:S(2)}, u32[]{:S(2)}) collective-permute-start(f32[8,256]{1,0:T(8,128)S(1)} %get-tuple-element.44), channel_id=1, source_target_pairs={{0,1},{2,3},{4,5},{6,7},{8,9},{10,11},{12,13},{14,15},{16,17},{18,... | collective-permute-start | bytes 24584 | tf_op jit(solution)/shard_map/ppermute | solution.py:225
  99.4 8.2 %collective-permute-start.5 = (f32[8,256]{1,0:T(8,128)S(1)}, f32[8,256]{1,0:T(8,128)S(1)}, u32[]{:S(2)}, u32[]{:S(2)}) collective-permute-start(f32[8,256]{1,0:T(8,128)S(1)} %get-tuple-element.45), channel_id=1, source_target_pairs={{1,2},{3,4},{5,6},{7,8},{9,10},{11,12},{13,14},{15,16},{17,18},{19... | collective-permute-start | bytes 24584 | tf_op jit(solution)/shard_map/ppermute | solution.py:225

commit v6 on v5

--- a/solution.py
+++ b/solution.py
@@ -229,12 +229,12 @@
     near = swap(jnp.where(is_odd, lower, upper), 0)
     own = corners + 8
     streamed = dict(scratch=(pltpu.VMEM(schur.shape, BF16), pltpu.SemaphoreType.DMA((width // RIM,))))
+    shapes = [
+        (corners, width), jax.ShapeDtypeStruct((corners, 1), jnp.int32), (1, LANES),
+        (own, RIM), (own, RIM), (N_COLS, 4, LANES), (cases, width),
+    ]
     scaled_basis, place, own_names, up_basis, down_basis, blocks, near_loads = call(
-        prepare_kernel,
-        [
-            (corners, width), jax.ShapeDtypeStruct((corners, 1), jnp.int32), (1, LANES),
-            (own, RIM), (own, RIM), (N_COLS, 4, LANES), (cases, width),
-        ],
+        prepare_kernel, shapes,
         *(in_place(x) for x in (basis, index[None], coarse_inverse, loads)), weights,
         in_hbm=(0, 1, 2, 3),
         scratch=(
@@ -262,7 +262,6 @@
         scratch=(pltpu.SemaphoreType.DMA((1,)),),
     )
     arrived = exchange(sent, COLS)
-    arrived, told_far, told_near = lax.optimization_barrier((arrived, told_far, told_near))
     (sent,) = call(
         block_kernel, [(N_ROWS, cases, LANES)], arrived, scratch=(pltpu.VMEM((4 * N_COLS, LANES), F32),)
     )

time: 109 us -> 104 us (0.954)
  blocking collectives: 30 us -> 60.1 us
  starting transfers between devices: 48.1 us -> 24.1 us
  waiting for transfers between devices: 20.3 us -> 9.9 us
    all_to_all x2 -> x3, blocking collectives: 30 us -> 60.1 us  [exchange(): return lax.all_to_all(x, axes, split_axis=0, concat_axis=0, tiled=True)]
    all_to_all x2 -> x1, starting transfers between devices: 25 us -> 3.81 us  [exchange(): return lax.all_to_all(x, axes, split_axis=0, concat_axis=0, tiled=True)]
    all_to_all x2 -> x1, waiting for transfers between devices: 9.88 us -> 0.01 us  [exchange(): return lax.all_to_all(x, axes, split_axis=0, concat_axis=0, tiled=True)]
    ppermute x6, starting transfers between devices: 23 us -> 20.3 us  [swap(): return lax.ppermute(x, CHAIN, pairs + [(j, i) for i, j in pairs])]
  transfers between devices with their start and end apart: 8 -> 7, of which waited for: 5 -> 4; matrix products, arithmetic and copies ran while one was open for 0% -> 0% of each run, Pallas kernels for 4% -> 4%
where the time goes in v6:
time: 104 us; the launch traced here: 103 us
  blocking collectives  60.1 us (58%)
  starting transfers between devices  24.1 us (23%)
  waiting for transfers between devices  9.9 us (10%)
  Pallas kernels  7.02 us (7%)
  other arithmetic  1.36 us (1%)
    all_to_all x3, blocking collectives, exchange(): return lax.all_to_all(x, axes, split_axis=0, concat_axis=0, tiled=True)  60.1 us
    ppermute x6, starting transfers between devices, swap(): return lax.ppermute(x, CHAIN, pairs + [(j, i) for i, j in pairs])  20.3 us
    ppermute x6, waiting for transfers between devices, swap(): return lax.ppermute(x, CHAIN, pairs + [(j, i) for i, j in pairs])  9.9 us
    pallas_call x8, Pallas kernels, call(): pl.pallas_call(kernel, out_shape=shapes, in_specs=[pl.BlockSpec(memory_sp...  7.02 us
    all_to_all x1, starting transfers between devices, exchange(): return lax.all_to_all(x, axes, split_axis=0, concat_axis=0, tiled=True)  3.81 us
  transfers between devices with their start and end apart: 7, of which 4 were waited for; matrix products, arithmetic and copies ran while one was open for 0% of the time, Pallas kernels for 4%

profile of v6, /device:TPU:24, one launch (start us, length us, event | category | flops | bytes accessed | tf_op | source)
XLA Modules:
  0.0 103.3 jit_solution(9654180854504075075)
XLA Ops:
  0.7 0.7 slice_select_fusion
  1.4 2.3 %collective-permute-start.1 = (f32[8,256]{1,0:T(8,128)S(1)}, f32[8,256]{1,0:T(8,128)S(1)}, u32[]{:S(2)}, u32[]{:S(2)}) collective-permute-start(f32[8,256]{1,0:T(8,128)S(1)} %get-tuple-element.42), channel_id=1, source_target_pairs={{0,1},{2,3},{4,5},{6,7},{8,9},{10,11},{12,13},{14,15},{16,17},{18,... | collective-permute-start | bytes 24584 | tf_op jit(solution)/shard_map/ppermute | solution.py:225
  3.7 5.1 %collective-permute-start = (f32[8,256]{1,0:T(8,128)S(1)}, f32[8,256]{1,0:T(8,128)S(1)}, u32[]{:S(2)}, u32[]{:S(2)}) collective-permute-start(f32[8,256]{1,0:T(8,128)S(1)} %get-tuple-element.43), channel_id=1, source_target_pairs={{1,2},{3,4},{5,6},{7,8},{9,10},{11,12},{13,14},{15,16},{17,18},{19... | collective-permute-start | bytes 24584 | tf_op jit(solution)/shard_map/ppermute | solution.py:225
  8.8 1.1 %shard_map.77 = (f32[24,1024]{1,0:T(8,128)S(1)}, s32[24,1]{1,0:T(8,128)S(1)}, f32[1,128]{1,0:T(1,128)S(1)}, f32[32,256]{1,0:T(8,128)S(1)}, f32[32,256]{1,0:T(8,1...) custom-call(f32[24,1024]{1,0:T(8,128)} %bitcast.9, s32[1,24]{1,0:T(1,128)} %index_from.1, ...), custom_call_target="tpu_custom_call" | custom-call | tf_op jit(solution)/shard_map/pallas_call | solution.py:201
  9.9 0.0 collective-permute-done.1.near
  9.9 2.0 %collective-permute-done.far = f32[8,256]{1,0:T(8,128)S(1)} collective-permute-done((f32[8,256]{1,0:T(8,128)S(1)}, f32[8,256]{1,0:T(8,128)S(1)}, u32[]{:S(2)}, u32[]{:S(2)}) %collective-permute-start) | collective-permute-done | bytes 8224 | tf_op jit(solution)/shard_map/ppermute | solution.py:225
  12.0 0.5 shard_map.78
  12.5 17.0 %all_to_all.20.arrived = f32[32,8,128]{2,1,0:T(8,128)S(1)} all-to-all(f32[32,8,128]{2,1,0:T(8,128)S(1)} %get-tuple-element.25), channel_id=1, replica_groups=mesh['yh'=2,'x'=4,'c'=2,'z'=12,'yl'=4] {'yh','x','yl'}, dimensions={0} | all-to-all | bytes 262144 | tf_op jit(solution)/shard_map/all_to_all | solution.py:27
  29.6 28.9 %all_to_all.21.arrived = f32[24,3,4,128]{3,2,1,0:T(4,128)S(1)} all-to-all(f32[24,3,4,128]{3,2,1,0:T(4,128)S(1)} %shard_map.79), channel_id=1, replica_groups=mesh['yh'=2,'x'=4,'c'=2,'z'=12,'yl'=4] {'z','c'}, dimensions={0} | all-to-all | bytes 294912 | tf_op jit(solution)/shard_map/all_to_all | solution.py:27
  58.5 0.2 shard_map.80
  58.7 14.2 %all_to_all.22.arrived = f32[32,8,128]{2,1,0:T(8,128)S(1)} all-to-all(f32[32,8,128]{2,1,0:T(8,128)S(1)} %shard_map.80), channel_id=1, replica_groups=mesh['yh'=2,'x'=4,'c'=2,'z'=12,'yl'=4] {'yh','x','yl'}, dimensions={0} | all-to-all | bytes 262144 | tf_op jit(solution)/shard_map/all_to_all | solution.py:27
  72.9 0.7 shard_map.81
  73.5 3.8 %all-to-all-start.3 = ((f32[24,8,128]{2,1,0:T(8,128)}), f32[24,8,128]{2,1,0:T(8,128)S(1)}, u32[]{:S(2)}, u32[]{:S(2)}) async-start(f32[24,8,128]{2,1,0:T(8,128)} %shard_map.81), calls=%async_computation.3 | async-start | bytes 196608 | tf_op jit(solution)/shard_map/all_to_all | solution.py:27
  77.4 1.7 %shard_map.82 = (f32[8,1024]{1,0:T(8,128)S(1)}, f32[40,256]{1,0:T(8,128)S(1)}, f32[40,256]{1,0:T(8,128)S(1)}) custom-call(f32[8,1024]{1,0:T(8,128)S(1)} %get-tuple-element.29.weighted, f32[1,1024]{1,0:T(1,128)S(1)} %or_select_fusion.weights, f32[1,256]{1,0:T(1,128)S(1)} %broadcast_in_dim.19.odd, f32[32,256]{1,0:T(8,128)S(1)} %get-tuple-element.30.up_basis, ...), custom_call_target="tpu_custom_call" | custom-call | tf_op jit(solution)/shard_map/pallas_call | solution.py:201
  79.1 6.3 %collective-permute-start.2 = (f32[40,256]{1,0:T(8,128)S(1)}, f32[40,256]{1,0:T(8,128)S(1)}, u32[]{:S(2)}, u32[]{:S(2)}) collective-permute-start(f32[40,256]{1,0:T(8,128)S(1)} %get-tuple-element.33), channel_id=1, source_target_pairs={{1,2},{3,4},{5,6},{7,8},{9,10},{11,12},{13,14},{15,16},{17,18},{19... | collective-permute-start | bytes 122888 | tf_op jit(solution)/shard_map/ppermute | solution.py:225
  85.4 1.9 %collective-permute-start.3 = (f32[40,256]{1,0:T(8,128)S(1)}, f32[40,256]{1,0:T(8,128)S(1)}, u32[]{:S(2)}, u32[]{:S(2)}) collective-permute-start(f32[40,256]{1,0:T(8,128)S(1)} %get-tuple-element.34), channel_id=1, source_target_pairs={{0,1},{2,3},{4,5},{6,7},{8,9},{10,11},{12,13},{14,15},{16,17},{18,... | collective-permute-start | bytes 122888 | tf_op jit(solution)/shard_map/ppermute | solution.py:225
  87.4 1.6 %shard_map.83.schur = bf16[1024,1024]{1,0:T(8,128)(2,1)S(1)} custom-call(bf16[1024,1024]{1,0:T(8,128)(2,1)} %bitcast.8), custom_call_target="tpu_custom_call" | custom-call | tf_op jit(solution)/shard_map/pallas_call | solution.py:201
  89.0 0.0 collective-permute-done.2.far
  89.0 2.3 %collective-permute-done.3.near = f32[40,256]{1,0:T(8,128)S(1)} collective-permute-done((f32[40,256]{1,0:T(8,128)S(1)}, f32[40,256]{1,0:T(8,128)S(1)}, u32[]{:S(2)}, u32[]{:S(2)}) %collective-permute-start.3) | collective-permute-done | bytes 40992 | tf_op jit(solution)/shard_map/ppermute | solution.py:225
  91.3 0.0 all-to-all-done.3.value
  91.3 1.2 %shard_map.84 = (f32[8,1024]{1,0:T(8,128)}, f32[8,1024]{1,0:T(8,128)S(1)}, f32[8,256]{1,0:T(8,128)S(1)}, f32[8,256]{1,0:T(8,128)S(1)}) custom-call(f32[24,8,128]{2,1,0:T(8,128)S(1)} %all-to-all-done.3.value, f32[1,128]{1,0:T(1,128)S(1)} %get-tuple-element.28.names, f32[24,1024]{1,0:T(8,128)S(1)} %get-tuple-element.22.scaled_basis, ...), custom_call_target="tpu_custom_call" | custom-call | tf_op jit(solution)/shard_map/pallas_call | solution.py:201
  92.5 1.9 %collective-permute-start.4 = (f32[8,256]{1,0:T(8,128)S(1)}, f32[8,256]{1,0:T(8,128)S(1)}, u32[]{:S(2)}, u32[]{:S(2)}) collective-permute-start(f32[8,256]{1,0:T(8,128)S(1)} %get-tuple-element.38), channel_id=1, source_target_pairs={{0,1},{2,3},{4,5},{6,7},{8,9},{10,11},{12,13},{14,15},{16,17},{18,... | collective-permute-start | bytes 24584 | tf_op jit(solution)/shard_map/ppermute | solution.py:225
  94.4 2.7 %collective-permute-start.5 = (f32[8,256]{1,0:T(8,128)S(1)}, f32[8,256]{1,0:T(8,128)S(1)}, u32[]{:S(2)}, u32[]{:S(2)}) collective-permute-start(f32[8,256]{1,0:T(8,128)S(1)} %get-tuple-element.39), channel_id=1, source_target_pairs={{1,2},{3,4},{5,6},{7,8},{9,10},{11,12},{13,14},{15,16},{17,18},{19... | collective-permute-start | bytes 24584 | tf_op jit(solution)/shard_map/ppermute | solution.py:225
  97.2 0.9 collective-permute-done.4
  98.0 4.6 %collective-permute-done.5 = f32[8,256]{1,0:T(8,128)S(1)} collective-permute-done((f32[8,256]{1,0:T(8,128)S(1)}, f32[8,256]{1,0:T(8,128)S(1)}, u32[]{:S(2)}, u32[]{:S(2)}) %collective-permute-start.5) | collective-permute-done | bytes 8224 | tf_op jit(solution)/shard_map/ppermute | solution.py:225
  102.7 0.6 fusion
  (5 shorter events, 0.1 us)
Async XLA Ops:
  1.4 8.5 %collective-permute-start.1 = (f32[8,256]{1,0:T(8,128)S(1)}, f32[8,256]{1,0:T(8,128)S(1)}, u32[]{:S(2)}, u32[]{:S(2)}) collective-permute-start(f32[8,256]{1,0:T(8,128)S(1)} %get-tuple-element.42), channel_id=1, source_target_pairs={{0,1},{2,3},{4,5},{6,7},{8,9},{10,11},{12,13},{14,15},{16,17},{18,... | collective-permute-start | bytes 24584 | tf_op jit(solution)/shard_map/ppermute | solution.py:225
  3.7 8.2 %collective-permute-start = (f32[8,256]{1,0:T(8,128)S(1)}, f32[8,256]{1,0:T(8,128)S(1)}, u32[]{:S(2)}, u32[]{:S(2)}) collective-permute-start(f32[8,256]{1,0:T(8,128)S(1)} %get-tuple-element.43), channel_id=1, source_target_pairs={{1,2},{3,4},{5,6},{7,8},{9,10},{11,12},{13,14},{15,16},{17,18},{19... | collective-permute-start | bytes 24584 | tf_op jit(solution)/shard_map/ppermute | solution.py:225
  73.5 17.8 %all-to-all-start.3 = ((f32[24,8,128]{2,1,0:T(8,128)}), f32[24,8,128]{2,1,0:T(8,128)S(1)}, u32[]{:S(2)}, u32[]{:S(2)}) async-start(f32[24,8,128]{2,1,0:T(8,128)} %shard_map.81), calls=%async_computation.3 | async-start | bytes 196608 | tf_op jit(solution)/shard_map/all_to_all | solution.py:27
  79.1 9.9 %collective-permute-start.2 = (f32[40,256]{1,0:T(8,128)S(1)}, f32[40,256]{1,0:T(8,128)S(1)}, u32[]{:S(2)}, u32[]{:S(2)}) collective-permute-start(f32[40,256]{1,0:T(8,128)S(1)} %get-tuple-element.33), channel_id=1, source_target_pairs={{1,2},{3,4},{5,6},{7,8},{9,10},{11,12},{13,14},{15,16},{17,18},{19... | collective-permute-start | bytes 122888 | tf_op jit(solution)/shard_map/ppermute | solution.py:225
  85.4 5.9 %collective-permute-start.3 = (f32[40,256]{1,0:T(8,128)S(1)}, f32[40,256]{1,0:T(8,128)S(1)}, u32[]{:S(2)}, u32[]{:S(2)}) collective-permute-start(f32[40,256]{1,0:T(8,128)S(1)} %get-tuple-element.34), channel_id=1, source_target_pairs={{0,1},{2,3},{4,5},{6,7},{8,9},{10,11},{12,13},{14,15},{16,17},{18,... | collective-permute-start | bytes 122888 | tf_op jit(solution)/shard_map/ppermute | solution.py:225
  92.5 5.5 %collective-permute-start.4 = (f32[8,256]{1,0:T(8,128)S(1)}, f32[8,256]{1,0:T(8,128)S(1)}, u32[]{:S(2)}, u32[]{:S(2)}) collective-permute-start(f32[8,256]{1,0:T(8,128)S(1)} %get-tuple-element.38), channel_id=1, source_target_pairs={{0,1},{2,3},{4,5},{6,7},{8,9},{10,11},{12,13},{14,15},{16,17},{18,... | collective-permute-start | bytes 24584 | tf_op jit(solution)/shard_map/ppermute | solution.py:225
  94.4 8.2 %collective-permute-start.5 = (f32[8,256]{1,0:T(8,128)S(1)}, f32[8,256]{1,0:T(8,128)S(1)}, u32[]{:S(2)}, u32[]{:S(2)}) collective-permute-start(f32[8,256]{1,0:T(8,128)S(1)} %get-tuple-element.39), channel_id=1, source_target_pairs={{1,2},{3,4},{5,6},{7,8},{9,10},{11,12},{13,14},{15,16},{17,18},{19... | collective-permute-start | bytes 24584 | tf_op jit(solution)/shard_map/ppermute | solution.py:225
